TPU v7x, 32 devices: a whole 2x2x4 slice. The times are simulated.
32 devices in a mesh: gx: 4 (over z), gy: 8 (over y, x, core).
Axes of the slice: x: 2, y: 2, z: 4, core: 2. Of those that a mesh axis runs over, the one named last changes fastest.
Arguments:
- child_dens: bfloat16 [296, 8192], P(None, ('gx', 'gy')), may hold values from -0.625 to 0.625
- users: int32 [2048], P(('gx', 'gy')), may hold values from 0 to 31
- local_dens: bfloat16 [296, 16384], P(None, ('gx', 'gy')), may hold values from -6 to 6
- live: int32 [32], P(('gx', 'gy')), may hold values from 16 to 128, as said below
- m2l_ops: bfloat16 [296, 2368], replicated, may hold values from -0.125 to 0.125
- m2l_lists: int32 [8, 4096], P(None, ('gx', 'gy')), may hold values from -1 to 143, as said below
- leaf_pos: float32 [3, 131072], P(None, ('gx', 'gy')), may hold values from 0 to 1
- leaf_charge: float32 [4, 131072], P(None, ('gx', 'gy')), may hold values from -0.2 to 0.2
- leaf_nbrs: int32 [4096, 27], P(('gx', 'gy')), may hold values from -1 to 159, as said below
Outputs:
- local_exp: float32 [296, 16384], P(None, ('gx', 'gy'))
- near_pot: float32 [4, 131072], P(None, ('gx', 'gy'))
Inputs may be any that keep to these rules, and one draw needn't show every extreme that they name: `live`: at least 16 on every device; some device has exactly 128. `m2l_lists`: entry for target slot k lies in k .. k + 16 or is -1. `leaf_nbrs`: entry for leaf l of a device lies in l .. l + 32 or is -1; the first entry is the leaf itself, l + 16.
All inputs are finite; a program needn't handle non-finite values.
Results may differ from a plain program's by a relative error of at most 0.00071.
Values may be sent and summed in bfloat16 or wider, within the bound.
A program may use at most 128 MiB of HBM per device.

v0:
```python
import jax
import jax.numpy as jnp
from jax import lax
from jax.sharding import PartitionSpec as P

Q = 4
NOFF = 8
SH_DEV = 1
NPT = 32
HL = 16


soften = 0.01


def extended_2(block, sides, width):
    for axis, dim in sides:
        count = lax.axis_size(axis)
        forward = [(i, i + 1) for i in range(count - 1)]
        backward = [(target, source) for source, target in forward]
        low = lax.ppermute(
            lax.slice_in_dim(block, block.shape[dim] - width, None, axis=dim), axis, forward
        )
        high = lax.ppermute(lax.slice_in_dim(block, 0, width, axis=dim), axis, backward)
        block = jnp.concatenate([low, block, high], axis=dim)
    return block


def partner(value, axis, apart):
    mask = 2**apart
    pairs = [(source, source ^ mask) for source in range(lax.axis_size(axis))]
    return lax.ppermute(value, axis, pairs)


def near_field(points, window, nbrs):
    span = window.shape[1]
    extended = jnp.concatenate(
        [window, jnp.zeros((window.shape[0], 1, window.shape[2]), jnp.float32)], axis=1
    )
    index = jnp.where(nbrs < 0, span, nbrs)
    source = jnp.take(extended, index, axis=1)
    source = source.reshape(source.shape[0], source.shape[1], -1)
    dist_sq = jnp.zeros((points.shape[1], points.shape[2], source.shape[2]), jnp.float32)
    for coord in range(3):
        diff = points[coord][:, :, None] - source[coord][:, None, :]
        dist_sq = dist_sq + diff * diff
    kernel = 1.0 / jnp.sqrt(dist_sq + soften)
    return jnp.einsum("lts,qls->qlt", kernel, source[3:], precision=lax.Precision.HIGHEST)


def per_device(
    child_dens, users, local_dens, live, m2l_ops, m2l_lists, leaf_pos, leaf_charge, leaf_nbrs
):
    surface = child_dens.shape[0]
    slots = local_dens.shape[1] // Q
    leaf_count = leaf_pos.shape[1] // NPT
    shared_total = SH_DEV * lax.axis_size("gx") * lax.axis_size("gy")
    points = jnp.concatenate([leaf_pos, leaf_charge], axis=0)
    wide_points = extended_2(points, ((("gx", "gy"), 1),), HL * NPT)
    near_pot = near_field(
        points.reshape(3 + Q, leaf_count, NPT)[:3],
        wide_points.reshape(3 + Q, leaf_count + 2 * HL, NPT),
        leaf_nbrs,
    )
    children = child_dens.reshape(surface, -1, Q)
    onehot = (users[:, None] == jnp.arange(shared_total, dtype=jnp.int32)[None, :]).astype(
        jnp.bfloat16
    )
    partial_value = jnp.einsum("pcq,cs->psq", children, onehot, preferred_element_type=jnp.float32)
    partial_value = partial_value.reshape(surface, shared_total * Q)
    block = partial_value
    high_rank = lax.axis_index("gx")
    for bit in range(lax.axis_size("gx").bit_length() - 2, -1, -1):
        half = block.shape[1] // 2
        upper = high_rank >> bit & 1 == 1
        keep = jnp.where(upper, block[:, half:], block[:, :half])
        give = jnp.where(upper, block[:, :half], block[:, half:])
        block = keep + partner(give, "gx", bit)
    low_rank = lax.axis_index("gy")
    for bit in range(lax.axis_size("gy").bit_length() - 2, -1, -1):
        half = block.shape[1] // 2
        upper = low_rank >> bit & 1 == 1
        keep = jnp.where(upper, block[:, half:], block[:, :half])
        give = jnp.where(upper, block[:, :half], block[:, half:])
        block = keep + partner(give, "gy", bit)
    own = local_dens.astype(jnp.float32).reshape(surface, slots, Q)
    own = own.at[:, :SH_DEV, :].add(block.reshape(surface, SH_DEV, Q))
    slot_ids = jnp.arange(slots, dtype=jnp.int32)
    lower = live[0] // 2
    upper_count = live[0] - lower
    alive = (slot_ids < lower) | (slot_ids >= slots - upper_count)
    owned = jnp.where(alive[None, :, None], own, jnp.float32(0.0)).astype(jnp.bfloat16)
    owned = owned.reshape(surface, slots * Q)
    rim = slots // 16
    window = extended_2(owned, ((("gx", "gy"), 1),), rim * Q)
    span = slots + 2 * rim
    extended = jnp.concatenate(
        [window.reshape(surface, span, Q), jnp.zeros((surface, 1, Q), jnp.bfloat16)], axis=1
    )
    index = jnp.where(m2l_lists < 0, span, m2l_lists)
    gathered = jnp.take(extended, index, axis=1)
    ops_blocks = m2l_ops.reshape(surface, NOFF, surface)
    expansion = jnp.einsum(
        "ioj,jotq->itq", ops_blocks, gathered, preferred_element_type=jnp.float32
    )
    expansion = jnp.where(alive[None, :, None], expansion, jnp.float32(0.0))
    local_exp = expansion.reshape(surface, slots * Q)
    return (local_exp, near_pot.reshape(Q, leaf_count * NPT))


def solution(mesh):
    placed = (
        P(None, ("gx", "gy")),
        P(("gx", "gy")),
        P(None, ("gx", "gy")),
        P(("gx", "gy")),
        P(),
        P(None, ("gx", "gy")),
        P(None, ("gx", "gy")),
        P(None, ("gx", "gy")),
        P(("gx", "gy"), None),
    )
    return jax.shard_map(
        per_device,
        mesh=mesh,
        in_specs=placed,
        out_specs=(P(None, ("gx", "gy")), P(None, ("gx", "gy"))),
        check_vma=False,
    )
```

profile of v0, /device:TPU:0, one launch (start us, length us, event | category | flops | bytes accessed | tf_op | source)
XLA Modules:
  0.0 152.9 jit_solution(5402965399107550629)
XLA Ops:
  0.6 1.1 copy.15
  1.7 0.1 reshape.111
  1.8 0.8 convolution_bitcast_fusion
  2.6 0.1 copy.17
  2.7 0.1 reshape.112
  2.8 4.1 %collective-permute-start = (f32[296,64]{0,1:T(8,128)S(1)}, f32[296,64]{0,1:T(8,128)S(1)}, u32[]{:S(2)}, u32[]{:S(2)}) collective-permute-start(f32[296,64]{0,1:T(8,128)S(1)} %slice_select_fusion), channel_id=1, source_target_pairs={{0,16},{8,24},{16,0},{24,8},{1,17},{9,25},{17,1},{25,9},{2,18},{10... | collective-permute-start | bytes 227336 | tf_op jit(solution)/shard_map/ppermute | solution.py:32
  7.0 0.8 pad_maximum_fusion.3
  7.7 1.5 collective-permute-start.7
  9.2 1.3 collective-permute-start.8
  11.2 0.7 bitcast_clamp_fusion
  11.9 1.3 compare_and_fusion.1
  13.1 0.7 compare_select_fusion
  13.8 0.7 compare_and_fusion
  14.6 1.1 slice_reduce_fusion.2
  15.7 0.1 copy.24
  15.8 0.2 reshape.132
  16.0 0.0 collective-permute-done
  16.1 6.3 %collective-permute-start.1 = (f32[296,32]{0,1:T(8,128)S(1)}, f32[296,32]{0,1:T(8,128)S(1)}, u32[]{:S(2)}, u32[]{:S(2)}) collective-permute-start(f32[296,32]{0,1:T(8,128)S(1)} %slice_select_fusion.1), channel_id=1, source_target_pairs={{0,8},{8,0},{16,24},{24,16},{1,9},{9,1},{17,25},{25,17},{2,10},{10... | collective-permute-start | bytes 113672 | tf_op jit(solution)/shard_map/ppermute | solution.py:32
  22.3 0.6 compare_or_fusion
  22.9 1.1 copy.14
  24.1 0.2 reshape.121
  24.3 3.8 %reshape.116 = bf16[296,8,296]{2,1,0:T(8,128)(2,1)S(1)} reshape(bf16[296,2368]{1,0:T(8,128)(2,1)} %param.15) | data formatting | bytes 2803712 | tf_op jit(solution)/shard_map/reshape | solution.py:102
  28.1 3.2 %copy.37 = bf16[296,8,296,1]{0,1,2,3:T(8,128)(2,1)} copy(bf16[296,8,296,1]{2,1,0,3:T(8,128)(2,1)S(1)} %bitcast.60) | data formatting | bytes 2803712 | tf_op jit(solution)/shard_map/reshape | solution.py:102
  31.3 0.1 copy.22
  31.4 0.1 sub.64
  31.5 0.1 sub.69
  31.6 0.1 sub.74
  31.7 0.0 collective-permute-done.1
  31.7 0.7 collective-permute-start.2
  32.4 0.9 pad_maximum_fusion.1
  33.3 0.2 reshape.118
  33.5 0.3 copy.23
  33.9 0.1 concatenate.21
  33.9 11.3 %gather_fusion.1 = f32[3456,7,32]{2,1,0:T(8,128)} fusion(f32[7,161,32]{2,0,1:T(8,128)S(1)} %concatenate.21, s32[4096]{0:T(1024)S(1)} %pad_clamp_fusion), kind=kCustom, calls=%fused_computation.1 | custom fusion | bytes 6206976 | tf_op jit(solution)/shard_map/jit(_take)/gather | solution.py:41
  45.3 18.4 %copy.42 = f32[128,27,7,32]{1,0,3,2:T(8,128)} copy(f32[128,27,7,32]{3,2,1,0:T(8,128)} %bitcast.59) | data formatting | bytes 6193152 | tf_op jit(solution)/shard_map/jit(_take)/gather | solution.py:41
  63.7 0.7 collective-permute-start.3
  64.4 13.7 %select_bitcast_fusion = f32[7,128,27,32]{2,1,3,0:T(8,128)} fusion(f32[128,27,7,32]{1,0,3,2:T(8,128)} %copy.42, pred[128,27]{1,0:T(8,128)(4,1)S(1)} %copy.22), kind=kLoop, calls=%fused_computation.2 | loop fusion | flops 774144 | bytes 6196608 | tf_op jit(solution)/shard_map/jit(_take)/select_n | solution.py:41
  78.1 0.6 slice_select_fusion.4
  78.7 5.5 %fusion.42 = (f32[1,128,27,32]{2,1,3,0:T(8,128)}, f32[1,128,27,32]{2,1,3,0:T(8,128)S(1)}, f32[1,128,27,32]{2,1,3,0:T(8,128)}) fusion(f32[7,128,27,32]{2,1,3,0:T(8,128)} %select_bitcast_fusion), kind=kLoop, calls=%fused_computation.65 | loop fusion | bytes 2654208 | tf_op jit(solution)/shard_map/slice | solution.py:45
  84.3 7.8 %slice.148 = f32[4,128,27,32]{2,1,3,0:T(8,128)} slice(f32[7,128,27,32]{2,1,3,0:T(8,128)} %select_bitcast_fusion), slice={[3:7], [0:128], [0:27], [0:32]} | slice | bytes 3538944 | tf_op jit(solution)/shard_map/slice | solution.py:48
  92.0 2.3 %copy.27 = f32[1,128,27,32]{1,3,2,0:T(8,128)S(1)} copy(f32[1,128,27,32]{2,1,3,0:T(8,128)} %get-tuple-element.19) | data formatting | bytes 884736 | tf_op jit(solution)/shard_map/slice | solution.py:45
  94.3 1.0 copy.28
  95.3 2.3 %copy.29 = f32[1,128,27,32]{1,3,2,0:T(8,128)S(1)} copy(f32[1,128,27,32]{2,1,3,0:T(8,128)} %get-tuple-element.21) | data formatting | bytes 884736 | tf_op jit(solution)/shard_map/slice | solution.py:45
  97.7 1.0 copy.30
  98.6 0.7 copy.31
  99.4 1.0 copy.32
  100.3 5.6 %copy.26 = f32[4,128,27,32]{1,3,2,0:T(8,128)S(1)} copy(f32[4,128,27,32]{2,1,3,0:T(8,128)} %slice.148) | data formatting | bytes 3538944 | tf_op jit(solution)/shard_map/slice | solution.py:48
  105.9 2.0 %copy.33 = f32[4,128,864]{2,0,1:T(4,128)} copy(f32[4,128,864]{1,2,0:T(8,128)S(1)} %bitcast.61) | data formatting | bytes 3538944 | tf_op jit(solution)/shard_map/slice | solution.py:48
  107.9 0.7 fusion.39
  108.6 0.9 select_convert_fusion
  109.6 0.2 reshape.114
  109.8 2.4 %collective-permute-start.5 = (bf16[296,32]{0,1:T(8,128)(2,1)S(1)}, bf16[296,32]{0,1:T(8,128)(2,1)S(1)}, u32[]{:S(2)}, u32[]{:S(2)}) collective-permute-start(bf16[296,32]{0,1:T(8,128)(2,1)S(1)} %get-tuple-element.22), channel_id=1, source_target_pairs={{0,1},{1,2},{2,3},{3,4},{4,5},{5,6},{6,7},{7,8},{8,9},{9,10},{10,1... | collective-permute-start | bytes 56840 | tf_op jit(solution)/shard_map/ppermute | solution.py:21
  112.2 1.5 collective-permute-start.6
  113.7 19.5 %fusion.32 = f32[4,128,32]{2,0,1:T(4,128)S(1)} fusion(f32[4,128,864]{2,0,1:T(4,128)} %copy.33, f32[128,864]{1,0:T(8,128)} %copy.32, f32[128,32]{1,0:T(8,128)S(1)} %sub.74, f32[128,864]{1,0:T(8,128)} %copy.30, f32[128,32]{1,0:T(8,128)S(1)} %sub.69, f32[128,864]{1,0:T(8,128)S(1)} %copy-done, f32[128,32]{1,0:T(8,128)S(1)} %sub.64), kind=kOutput, calls=%fused_computation.29 | convolution fusion | flops 201719808 | bytes 3211264 | tf_op jit(solution)/shard_map/lts,qls->qlt/dot_general | solution.py:48
  133.2 0.8 reshape.119
  134.0 0.1 pad_maximum_fusion
  134.1 0.1 reshape.115
  134.2 0.2 concatenate.18
  134.4 9.9 %gather_fusion = bf16[1024,296,4]{1,2,0:T(4,128)(2,1)} fusion(bf16[296,145,4]{0,2,1:T(4,128)(2,1)S(1)} %concatenate.18, s32[1024]{0:T(1024)S(1)} %bitcast_clamp_fusion), kind=kCustom, calls=%fused_computation | custom fusion | bytes 4853760 | tf_op jit(solution)/shard_map/jit(_take)/gather | solution.py:101
  144.4 4.3 %copy.39 = bf16[8,128,296,4]{1,0,2,3:T(8,128)(2,1)S(1)} copy(bf16[8,128,296,4]{2,3,1,0:T(4,128)(2,1)} %bitcast.58) | data formatting | bytes 4849664 | tf_op jit(solution)/shard_map/jit(_take)/gather | solution.py:101
  148.7 2.5 %fusion.29 = f32[296,128,4]{1,0,2:T(8,128)S(1)} fusion(bf16[296,8,296,1]{0,1,2,3:T(8,128)(2,1)} %copy.37, bf16[8,128,296,4]{1,0,2,3:T(8,128)(2,1)S(1)} %copy.39, pred[8,128]{1,0:T(8,128)(4,1)S(1)} %copy-done.1, pred[128]{0:T(512)(128)(4,1)S(1)} %copy-done.2), kind=kOutput, calls=%fused_computation.28 | convolution fusion | flops 719114240 | bytes 4434048 | tf_op jit(solution)/shard_map/ioj,jotq->itq/dot_general | solution.py:103
  151.2 0.3 copy.21
  151.5 0.3 reshape.117
  151.8 1.1 copy.35
  (25 shorter events, 0.2 us)
Async XLA Ops:
  2.8 13.2 %collective-permute-start = (f32[296,64]{0,1:T(8,128)S(1)}, f32[296,64]{0,1:T(8,128)S(1)}, u32[]{:S(2)}, u32[]{:S(2)}) collective-permute-start(f32[296,64]{0,1:T(8,128)S(1)} %slice_select_fusion), channel_id=1, source_target_pairs={{0,16},{8,24},{16,0},{24,8},{1,17},{9,25},{17,1},{25,9},{2,18},{10... | collective-permute-start | bytes 227336 | tf_op jit(solution)/shard_map/ppermute | solution.py:32
  7.7 24.7 %collective-permute-start.7 = (f32[7,512]{1,0:T(8,128)S(1)}, f32[7,512]{1,0:T(8,128)S(1)}, u32[]{:S(2)}, u32[]{:S(2)}) collective-permute-start(f32[7,512]{1,0:T(8,128)S(1)} %get-tuple-element.24), channel_id=1, source_target_pairs={{0,1},{1,2},{2,3},{3,4},{4,5},{5,6},{6,7},{7,8},{8,9},{9,10},{10,1... | collective-permute-start | bytes 43016 | tf_op jit(solution)/shard_map/ppermute | solution.py:21
  9.2 23.2 %collective-permute-start.8 = (f32[7,512]{1,0:T(8,128)S(1)}, f32[7,512]{1,0:T(8,128)S(1)}, u32[]{:S(2)}, u32[]{:S(2)}) collective-permute-start(f32[7,512]{1,0:T(8,128)S(1)} %get-tuple-element.25), channel_id=1, source_target_pairs={{1,0},{2,1},{3,2},{4,3},{5,4},{6,5},{7,6},{8,7},{9,8},{10,9},{11,1... | collective-permute-start | bytes 43016 | tf_op jit(solution)/shard_map/ppermute | solution.py:24
  16.1 15.6 %collective-permute-start.1 = (f32[296,32]{0,1:T(8,128)S(1)}, f32[296,32]{0,1:T(8,128)S(1)}, u32[]{:S(2)}, u32[]{:S(2)}) collective-permute-start(f32[296,32]{0,1:T(8,128)S(1)} %slice_select_fusion.1), channel_id=1, source_target_pairs={{0,8},{8,0},{16,24},{24,16},{1,9},{9,1},{17,25},{25,17},{2,10},{10... | collective-permute-start | bytes 113672 | tf_op jit(solution)/shard_map/ppermute | solution.py:32
  31.7 32.0 %collective-permute-start.2 = (f32[296,16]{0,1:T(8,128)S(1)}, f32[296,16]{0,1:T(8,128)S(1)}, u32[]{:S(2)}, u32[]{:S(2)}) collective-permute-start(f32[296,16]{0,1:T(8,128)S(1)} %slice_select_fusion.2), channel_id=1, source_target_pairs={{0,4},{1,5},{2,6},{3,7},{4,0},{5,1},{6,2},{7,3},{8,12},{9,13},{10,... | collective-permute-start | bytes 56840 | tf_op jit(solution)/shard_map/ppermute | solution.py:32
  63.7 14.4 %collective-permute-start.3 = (f32[296,8]{0,1:T(8,128)S(1)}, f32[296,8]{0,1:T(8,128)S(1)}, u32[]{:S(2)}, u32[]{:S(2)}) collective-permute-start(f32[296,8]{0,1:T(8,128)S(1)} %slice_select_fusion.3), channel_id=1, source_target_pairs={{0,2},{1,3},{2,0},{3,1},{4,6},{5,7},{6,4},{7,5},{8,10},{9,11},{10,... | collective-permute-start | bytes 28424 | tf_op jit(solution)/shard_map/ppermute | solution.py:32
  78.7 29.2 %collective-permute-start.4 = (f32[296,4]{0,1:T(4,128)}, f32[296,4]{0,1:T(4,128)}, u32[]{:S(2)}, u32[]{:S(2)}) collective-permute-start(f32[296,4]{0,1:T(4,128)} %slice_select_fusion.4), channel_id=1, source_target_pairs={{0,1},{1,0},{2,3},{3,2},{4,5},{5,4},{6,7},{7,6},{8,9},{9,8},{10,11... | collective-permute-start | bytes 14216 | tf_op jit(solution)/shard_map/ppermute | solution.py:32
  100.3 13.3 %copy-start = (f32[128,864]{1,0:T(8,128)S(1)}, f32[128,864]{1,0:T(8,128)}, u32[]{:S(2)}) copy-start(f32[128,864]{1,0:T(8,128)} %copy.28) | copy-start | bytes 1327108
  109.8 24.2 %collective-permute-start.5 = (bf16[296,32]{0,1:T(8,128)(2,1)S(1)}, bf16[296,32]{0,1:T(8,128)(2,1)S(1)}, u32[]{:S(2)}, u32[]{:S(2)}) collective-permute-start(bf16[296,32]{0,1:T(8,128)(2,1)S(1)} %get-tuple-element.22), channel_id=1, source_target_pairs={{0,1},{1,2},{2,3},{3,4},{4,5},{5,6},{6,7},{7,8},{8,9},{9,10},{10,1... | collective-permute-start | bytes 56840 | tf_op jit(solution)/shard_map/ppermute | solution.py:21
  112.2 21.8 %collective-permute-start.6 = (bf16[296,32]{0,1:T(8,128)(2,1)S(1)}, bf16[296,32]{0,1:T(8,128)(2,1)S(1)}, u32[]{:S(2)}, u32[]{:S(2)}) collective-permute-start(bf16[296,32]{0,1:T(8,128)(2,1)S(1)} %get-tuple-element.23), channel_id=1, source_target_pairs={{1,0},{2,1},{3,2},{4,3},{5,4},{6,5},{7,6},{8,7},{9,8},{10,9},{11,1... | collective-permute-start | bytes 56840 | tf_op jit(solution)/shard_map/ppermute | solution.py:24
  134.4 14.2 %copy-start.1 = (pred[8,128]{1,0:T(8,128)(4,1)S(1)}, pred[8,128]{1,0:T(8,128)(4,1)}, u32[]{:S(2)}) copy-start(pred[8,128]{1,0:T(8,128)(4,1)} %compare_and_fusion.1) | copy-start | bytes 3076
  134.4 14.2 %copy-start.2 = (pred[128]{0:T(512)(128)(4,1)S(1)}, pred[128]{0:T(512)(128)(4,1)}, u32[]{:S(2)}) copy-start(pred[128]{0:T(512)(128)(4,1)} %compare_or_fusion) | copy-start | bytes 388
where the time goes:
time: 155 us; the launch traced here: 153 us
  local copies, waits for them, and re-layouts  88.2 us (57%)
  matrix products  22.8 us (15%)
  other arithmetic  21.8 us (14%)
  starting transfers between devices  18.4 us (12%)
  between operations  1.68 us (1%)
    gather x2, local copies, waits for them, and re-layouts, near_field(): source = jnp.take(extended, index, axis=1)  29.8 us
    dot_general x1, matrix products, near_field(): jnp.einsum('lts,qls->qlt', kernel, source[3:], precision=lax.Precision.HI...  19.5 us
    slice x3, local copies, waits for them, and re-layouts, near_field(): source[3:]  15.3 us
    select_n x2, other arithmetic, near_field(): source = jnp.take(extended, index, axis=1)  14.4 us
    gather x2, local copies, waits for them, and re-layouts, per_device(): gathered = jnp.take(extended, index, axis=1)  14.2 us
    slice x5, local copies, waits for them, and re-layouts, near_field(): diff = points[coord][:, :, None] - source[coord][:, None, :]  12 us
    ppermute x5, starting transfers between devices, partner(): return lax.ppermute(value, axis, pairs)  11.7 us
    reshape x2, local copies, waits for them, and re-layouts, per_device(): ops_blocks = m2l_ops.reshape(surface, NOFF, surface)  7.01 us
  transfers between devices with their start and end apart: 9, of which 0 were waited for; matrix products, arithmetic and copies ran while one was open for 72% of the time, Pallas kernels for 0%

commit v1 on v0

v1 whole, which is shorter than its diff:
```python
import jax
import jax.numpy as jnp
from jax import lax
from jax.experimental import pallas as pl
from jax.experimental.pallas import tpu as pltpu
from jax.sharding import PartitionSpec as P

Q = 4
NOFF = 8
SH_DEV = 1
NPT = 32
HL = 16
GROUP = 4
BLOCK = 32

soften = 0.01
f32 = jnp.float32
bf16 = jnp.bfloat16


def extended_2(block, sides, width):
    for axis, dim in sides:
        count = lax.axis_size(axis)
        forward = [(i, i + 1) for i in range(count - 1)]
        backward = [(target, source) for source, target in forward]
        low = lax.ppermute(
            lax.slice_in_dim(block, block.shape[dim] - width, None, axis=dim), axis, forward
        )
        high = lax.ppermute(lax.slice_in_dim(block, 0, width, axis=dim), axis, backward)
    return low, high


def partner(value, axis, apart):
    mask = 2**apart
    pairs = [(source, source ^ mask) for source in range(lax.axis_size(axis))]
    return lax.ppermute(value, axis, pairs)


def split3(value):
    first = value.astype(bf16).astype(f32)
    rest = value - first
    second = rest.astype(bf16).astype(f32)
    return first, second, rest - second


def row_ids(shape):
    return lax.broadcasted_iota(jnp.int32, shape, 0)


def lane_ids(shape):
    return lax.broadcasted_iota(jnp.int32, shape, 1)


def with_norm(coords):
    norm = jnp.sum(coords * coords, axis=0, keepdims=True)
    return jnp.where(row_ids(coords.shape) == 3, norm, coords), norm


def source_rows(coords):
    value, _ = with_norm(coords)
    one, two, three = split3(value)
    flat = jnp.where(row_ids(value.shape) < 3, f32(1.0), f32(0.0))
    return jnp.concatenate(
        [one, two, three, one, two, one, flat, jnp.zeros_like(one)], axis=0
    ).astype(bf16)


def target_rows(coords):
    value, norm = with_norm(coords)
    one, two, three = split3(value)
    row = row_ids(value.shape)
    main = jnp.where(row < 3, -2.0 * one, jnp.where(row == 3, f32(1.0), f32(0.0)))
    second = jnp.where(row < 3, -2.0 * two, f32(0.0))
    third = jnp.where(row < 3, -2.0 * three, f32(0.0))
    part = split3(norm + soften)
    flat = jnp.where(
        row == 0,
        part[0],
        jnp.where(row == 1, part[1], jnp.where(row == 2, part[2], f32(0.0))),
    )
    return jnp.concatenate(
        [main, main, main, second, second, third, flat, jnp.zeros_like(one)], axis=0
    ).astype(bf16)


def near_counts(nbrs, counts):
    slots, leaves = nbrs.shape
    groups, eight, reach = counts.shape
    span = GROUP + 2 * HL
    rows = -(-span // 16) * 16
    base = nbrs - lane_ids(nbrs.shape) // GROUP * GROUP
    base = jnp.where(nbrs < 0, -1, base)
    ids = row_ids((rows, leaves))
    total = jnp.zeros((rows, leaves), f32)
    for j in range(slots):
        total = total + jnp.where(ids == base[j : j + 1, :], f32(1.0), f32(0.0))
    wide = groups * eight
    lane = lane_ids((leaves, wide))
    twice = row_ids((leaves, wide)) == lane // 8 * GROUP + lane % GROUP
    doubled = jnp.dot(
        total.astype(bf16), jnp.where(twice, f32(1.0), f32(0.0)).astype(bf16),
        preferred_element_type=f32,
    )
    spread = row_ids((rows, reach)) == lane_ids((rows, reach)) // NPT
    full = lax.dot_general(
        doubled.T.astype(bf16),
        jnp.where(spread, f32(1.0), f32(0.0)).astype(bf16),
        (((1,), (0,)), ((), ())),
        preferred_element_type=f32,
    )
    counts[...] = full.reshape(groups, eight, reach)


def near_group(g, sources, targets, charges, counts, out):
    reach = counts.shape[2]
    size = GROUP * NPT
    start = pl.multiple_of(g * size, size)
    left = targets[pl.ds(start, size), :]
    cnt = counts[g]
    half = row_ids(cnt.shape) < GROUP
    ch = charges[:, pl.ds(start, reach)]
    w = jnp.concatenate(
        [cnt * jnp.where(half, ch[p : p + 1], ch[p + 1 : p + 2]) for p in range(0, Q, 2)],
        axis=0,
    )
    wh = w.astype(bf16)
    wl = (w - wh.astype(f32)).astype(bf16)
    w = jnp.concatenate([wh, wl], axis=0)
    acc = jnp.zeros((size, w.shape[0]), f32)
    nt = (((1,), (1,)), ((), ()))
    for at in range(0, reach, 256):
        width = min(256, reach - at)
        right = sources[:, pl.ds(pl.multiple_of(start + at, size), width)]
        dist = jnp.dot(left, right, preferred_element_type=f32)
        kernel = lax.rsqrt(dist)
        high = kernel.astype(bf16)
        low = (kernel - high.astype(f32)).astype(bf16)
        part = w[:, at : at + width]
        acc = acc + lax.dot_general(high, part, nt, preferred_element_type=f32)
        acc = acc + lax.dot_general(low, part, nt, preferred_element_type=f32)
    flat = acc.T
    rows = Q * GROUP
    flat = flat[:rows] + flat[rows:]
    mine = row_ids(flat.shape) % GROUP == lane_ids(flat.shape) // NPT
    flat = jnp.where(mine, flat, f32(0.0))
    out[:, pl.ds(start, size)] = jnp.sum(flat.reshape(Q, GROUP, size), axis=1)


def near_kernel(
    pos, charge, low, high, nbrs, out, coords, charges, sources, targets, counts
):
    halo = low.shape[1]
    count = pos.shape[1]
    coords[...] = jnp.zeros_like(coords)
    for ref, at in ((low, 0), (high, halo + count)):
        coords[0:3, at : at + halo] = ref[0:3, :]
        charges[:, at : at + halo] = ref[3:, :]
    coords[0:3, halo : halo + count] = pos[...]
    charges[:, halo : halo + count] = charge[...]
    sources[...] = source_rows(coords[...])
    targets[...] = target_rows(coords[:, halo : halo + count]).T
    near_counts(nbrs[...], counts)
    groups = counts.shape[0]

    def step(g, carry):
        near_group(g, sources, targets, charges, counts, out)
        return carry

    lax.fori_loop(0, groups, step, 0)


def near_field(pos, charge, low, high, nbrs):
    count = pos.shape[1]
    halo = low.shape[1]
    leaves = count // NPT
    groups = leaves // GROUP
    span = count + 2 * halo
    reach = (GROUP + 2 * HL) * NPT
    return pl.pallas_call(
        near_kernel,
        out_shape=jax.ShapeDtypeStruct(charge.shape, f32),
        scratch_shapes=[
            pltpu.VMEM((8, span), f32),
            pltpu.VMEM((Q, span), f32),
            pltpu.VMEM((64, span), bf16),
            pltpu.VMEM((count, 64), bf16),
            pltpu.VMEM((groups, 8, reach), f32),
        ],
    )(pos, charge, low, high, nbrs.T)


def alive_lanes(live, slots, shape):
    slot = lane_ids(shape) // Q
    lower = live // 2
    return (slot < lower) | (slot >= slots - (live - lower))


def m2l_gather(window, lists, gathered):
    offsets, slots = lists.shape
    surface = window.shape[0]
    wide = slots * Q
    expand = row_ids((slots, wide)) == lane_ids((slots, wide)) // Q
    place = jnp.dot(
        (lists + 1).astype(f32).astype(bf16),
        jnp.where(expand, f32(1.0), f32(0.0)).astype(bf16),
        preferred_element_type=f32,
    ).astype(jnp.int32)
    place = (place - 1) * Q + lane_ids(place.shape) % Q
    size = BLOCK * Q
    depth = (BLOCK + slots // 8) * Q
    for b in range(slots // BLOCK):
        block = window[:, b * size : b * size + depth]
        ids = row_ids((depth, size)) + b * size
        for o in range(0, offsets, 2):
            pair = []
            for k in (o, o + 1):
                hit = ids == place[k : k + 1, b * size : (b + 1) * size]
                hot = jnp.where(hit, f32(1.0), f32(0.0)).astype(bf16)
                pair.append(jnp.dot(block, hot, preferred_element_type=f32))
            both = jnp.concatenate(pair, axis=0).astype(bf16)
            gathered[o * surface : (o + 2) * surface, b * size : (b + 1) * size] = both


def m2l_kernel(live, owned, low, high, lists, ops, out, window, gathered):
    wide = owned.shape[1]
    rim = low.shape[1]
    slots = wide // Q
    window[:, 0:rim] = low[...]
    window[:, rim : rim + wide] = owned[...]
    window[:, rim + wide :] = high[...]
    m2l_gather(window, lists[...], gathered)
    result = jnp.dot(ops[...], gathered[...], preferred_element_type=f32)
    alive = alive_lanes(live[0], slots, result.shape)
    out[...] = jnp.where(alive, result, f32(0.0))


def m2l(live, owned, low, high, lists, ops):
    surface, wide = owned.shape
    vmem = pl.BlockSpec(memory_space=pltpu.VMEM)
    return pl.pallas_call(
        m2l_kernel,
        out_shape=jax.ShapeDtypeStruct((surface, wide), f32),
        in_specs=[pl.BlockSpec(memory_space=pltpu.SMEM)] + [vmem] * 5,
        scratch_shapes=[
            pltpu.VMEM((surface, wide + 2 * low.shape[1]), bf16),
            pltpu.VMEM((surface * lists.shape[0], wide), bf16),
        ],
    )(live, owned, low, high, lists, ops)


def per_device(
    child_dens, users, local_dens, live, m2l_ops, m2l_lists, leaf_pos, leaf_charge, leaf_nbrs
):
    surface = child_dens.shape[0]
    slots = local_dens.shape[1] // Q
    shared_total = SH_DEV * lax.axis_size("gx") * lax.axis_size("gy")
    halo = HL * NPT
    tail = jnp.concatenate([leaf_pos[:, -halo:], leaf_charge[:, -halo:]], axis=0)
    head = jnp.concatenate([leaf_pos[:, :halo], leaf_charge[:, :halo]], axis=0)
    low, high = extended_2(jnp.concatenate([head, tail], axis=1), ((("gx", "gy"), 1),), halo)
    near_pot = near_field(leaf_pos, leaf_charge, low, high, leaf_nbrs)
    children = child_dens.reshape(surface, -1, Q)
    onehot = (users[:, None] == jnp.arange(shared_total, dtype=jnp.int32)[None, :]).astype(
        jnp.bfloat16
    )
    partial_value = jnp.einsum("pcq,cs->psq", children, onehot, preferred_element_type=jnp.float32)
    block = partial_value.reshape(surface, shared_total * Q)
    high_rank = lax.axis_index("gx")
    for bit in range(lax.axis_size("gx").bit_length() - 2, -1, -1):
        half = block.shape[1] // 2
        upper = high_rank >> bit & 1 == 1
        keep = jnp.where(upper, block[:, half:], block[:, :half])
        give = jnp.where(upper, block[:, :half], block[:, half:])
        block = keep + partner(give, "gx", bit)
    low_rank = lax.axis_index("gy")
    for bit in range(lax.axis_size("gy").bit_length() - 2, -1, -1):
        half = block.shape[1] // 2
        upper = low_rank >> bit & 1 == 1
        keep = jnp.where(upper, block[:, half:], block[:, :half])
        give = jnp.where(upper, block[:, :half], block[:, half:])
        block = keep + partner(give, "gy", bit)
    first = SH_DEV * Q
    own = local_dens.astype(jnp.float32)
    own = jnp.concatenate([own[:, :first] + block, own[:, first:]], axis=1)
    slot_ids = jnp.arange(slots * Q, dtype=jnp.int32) // Q
    lower = live[0] // 2
    upper_count = live[0] - lower
    alive = (slot_ids < lower) | (slot_ids >= slots - upper_count)
    owned = jnp.where(alive[None, :], own, jnp.float32(0.0)).astype(jnp.bfloat16)
    rim = slots // 16 * Q
    wlow, whigh = extended_2(owned, ((("gx", "gy"), 1),), rim)
    local_exp = m2l(live, owned, wlow, whigh, m2l_lists, m2l_ops)
    return (local_exp, near_pot)


def solution(mesh):
    placed = (
        P(None, ("gx", "gy")),
        P(("gx", "gy")),
        P(None, ("gx", "gy")),
        P(("gx", "gy")),
        P(),
        P(None, ("gx", "gy")),
        P(None, ("gx", "gy")),
        P(None, ("gx", "gy")),
        P(("gx", "gy"), None),
    )
    return jax.shard_map(
        per_device,
        mesh=mesh,
        in_specs=placed,
        out_specs=(P(None, ("gx", "gy")), P(None, ("gx", "gy"))),
        check_vma=False,
    )
```

time: 155 us -> 75.8 us (0.49)
  the two profiles are of different devices: /device:TPU:0 before, /device:TPU:23 now
where the time goes in v1:
time: 75.8 us; the launch traced here: 75.4 us
  Pallas kernels  29.1 us (38%)
  starting transfers between devices  20 us (26%)
  waiting for transfers between devices  17.7 us (23%)
  local copies, waits for them, and re-layouts  5.09 us (7%)
  between operations  1.58 us (2%)
  other arithmetic  1.14 us (2%)
  matrix products  0.81 us (1%)
    pallas_call x1, Pallas kernels, near_field(): pl.pallas_call(near_kernel, out_shape=jax.ShapeDtypeStruct(charge.shape,...  24.2 us
    ppermute x5, waiting for transfers between devices, partner(): return lax.ppermute(value, axis, pairs)  13.6 us
    ppermute x2, starting transfers between devices, extended_2(): lax.ppermute(lax.slice_in_dim(block, block.shape[dim] - width, None, axis...  9.23 us
    ppermute x5, starting transfers between devices, partner(): return lax.ppermute(value, axis, pairs)  6.11 us
    pallas_call x1, Pallas kernels, m2l(): pl.pallas_call(m2l_kernel, out_shape=jax.ShapeDtypeStruct((surface, wide)...  4.82 us
    ppermute x2, starting transfers between devices, extended_2(): lax.ppermute(lax.slice_in_dim(block, 0, width, axis=dim), axis, backward)  4.61 us
    ppermute x2, waiting for transfers between devices, extended_2(): lax.ppermute(lax.slice_in_dim(block, 0, width, axis=dim), axis, backward)  4.14 us
    unnamed x15, local copies, waits for them, and re-layouts  3.12 us
  transfers between devices with their start and end apart: 9, of which 5 were waited for; matrix products, arithmetic and copies ran while one was open for 3% of the time, Pallas kernels for 32%

profile of v1, /device:TPU:23, one launch (start us, length us, event | category | flops | bytes accessed | tf_op | source)
XLA Modules:
  0.0 75.4 jit_solution(6472627485749186826)
XLA Ops:
  0.6 1.1 %copy.13 = bf16[296,256]{0,1:T(8,128)(2,1)S(1)} copy(bf16[296,256]{1,0:T(8,128)(2,1)} %param.9) | data formatting | bytes 303104 | tf_op args[0]
  1.7 0.1 reshape.27
  1.8 0.8 %convolution_bitcast_fusion = f32[296,32,4]{0,1,2:T(8,128)S(1)} fusion(bf16[296,64,4]{0,2,1:T(4,128)(2,1)S(1)} %reshape.27, s32[64]{0:T(128)} %param.10), kind=kOutput, calls=%fused_computation | convolution fusion | flops 4851712 | bytes 303360 | tf_op jit(solution)/shard_map/pcq,cs->psq/dot_general | solution.py:266
  2.6 0.1 copy.15
  2.7 0.1 reshape.28
  2.8 0.1 copy.18
  3.0 0.1 copy.19
  3.1 0.1 collective-permute-start
  3.2 5.9 %collective-permute-done = f32[296,64]{1,0:T(8,128)S(1)} collective-permute-done((f32[296,64]{1,0:T(8,128)S(1)}, f32[296,64]{1,0:T(8,128)S(1)}, u32[]{:S(2)}, u32[]{:S(2)}) %collective-permute-start) | collective-permute-done | bytes 75808 | tf_op jit(solution)/shard_map/ppermute | solution.py:36
  9.1 0.1 slice_select_fusion.3
  9.3 5.3 %collective-permute-start.1 = (f32[296,32]{1,0:T(8,128)S(1)}, f32[296,32]{1,0:T(8,128)S(1)}, u32[]{:S(2)}, u32[]{:S(2)}) collective-permute-start(f32[296,32]{1,0:T(8,128)S(1)} %slice_select_fusion.3), channel_id=1, source_target_pairs={{0,8},{8,0},{16,24},{24,16},{1,9},{9,1},{17,25},{25,17},{2,10},{10... | collective-permute-start | bytes 113672 | tf_op jit(solution)/shard_map/ppermute | solution.py:36
  14.6 0.7 fusion.13
  15.3 3.1 %collective-permute-done.1 = f32[296,32]{1,0:T(8,128)S(1)} collective-permute-done((f32[296,32]{1,0:T(8,128)S(1)}, f32[296,32]{1,0:T(8,128)S(1)}, u32[]{:S(2)}, u32[]{:S(2)}) %collective-permute-start.1) | collective-permute-done | bytes 37920 | tf_op jit(solution)/shard_map/ppermute | solution.py:36
  18.4 0.1 select_add_fusion.2
  18.5 0.0 copy-start.1
  18.5 0.1 slice_select_fusion.2
  18.6 0.3 collective-permute-start.2
  18.9 0.7 fusion.14
  19.6 3.5 %collective-permute-done.2 = f32[296,16]{1,0:T(8,128)S(1)} collective-permute-done((f32[296,16]{1,0:T(8,128)S(1)}, f32[296,16]{1,0:T(8,128)S(1)}, u32[]{:S(2)}, u32[]{:S(2)}) %collective-permute-start.2) | collective-permute-done | bytes 18976 | tf_op jit(solution)/shard_map/ppermute | solution.py:36
  23.1 0.1 select_add_fusion.1
  23.2 0.1 slice_select_fusion.1
  23.3 0.3 collective-permute-start.3
  23.7 6.2 %collective-permute-start.7 = (f32[7,512]{1,0:T(8,128)S(1)}, f32[7,512]{1,0:T(8,128)S(1)}, u32[]{:S(2)}, u32[]{:S(2)}) collective-permute-start(f32[7,512]{1,0:T(8,128)S(1)} %pad_maximum_fusion), channel_id=1, source_target_pairs={{0,1},{1,2},{2,3},{3,4},{4,5},{5,6},{6,7},{7,8},{8,9},{9,10},{10,1... | collective-permute-start | bytes 43016 | tf_op jit(solution)/shard_map/ppermute | solution.py:26
  30.6 0.0 collective-permute-done.3
  30.6 0.1 select_add_fusion
  30.7 0.1 slice_select_fusion
  30.8 0.1 collective-permute-start.4
  30.9 0.0 copy-done.1
  30.9 0.1 convert_element_type.7
  31.0 0.2 slice.93
  31.1 1.1 %collective-permute-done.4 = f32[296,4]{1,0:T(8,128)S(1)} collective-permute-done((f32[296,4]{1,0:T(8,128)S(1)}, f32[296,4]{1,0:T(8,128)S(1)}, u32[]{:S(2)}, u32[]{:S(2)}) %collective-permute-start.4) | collective-permute-done | bytes 4768 | tf_op jit(solution)/shard_map/ppermute | solution.py:36
  32.2 0.1 slice_add_fusion
  32.4 0.2 fusion.owned
  32.5 0.0 copy-start
  32.5 0.1 fusion.11
  32.6 3.0 %collective-permute-start.5 = (bf16[296,32]{1,0:T(8,128)(2,1)S(1)}, bf16[296,32]{1,0:T(8,128)(2,1)S(1)}, u32[]{:S(2)}, u32[]{:S(2)}) collective-permute-start(bf16[296,32]{1,0:T(8,128)(2,1)S(1)} %get-tuple-element.3), channel_id=1, source_target_pairs={{0,1},{1,2},{2,3},{3,4},{4,5},{5,6},{6,7},{7,8},{8,9},{9,10},{10,1... | collective-permute-start | bytes 56840 | tf_op jit(solution)/shard_map/ppermute | solution.py:26
  35.6 1.9 %collective-permute-start.6 = (bf16[296,32]{1,0:T(8,128)(2,1)S(1)}, bf16[296,32]{1,0:T(8,128)(2,1)S(1)}, u32[]{:S(2)}, u32[]{:S(2)}) collective-permute-start(bf16[296,32]{1,0:T(8,128)(2,1)S(1)} %get-tuple-element.2), channel_id=1, source_target_pairs={{1,0},{2,1},{3,2},{4,3},{5,4},{6,5},{7,6},{8,7},{9,8},{10,9},{11,1... | collective-permute-start | bytes 56840 | tf_op jit(solution)/shard_map/ppermute | solution.py:29
  37.6 2.7 %collective-permute-start.8 = (f32[7,512]{1,0:T(8,128)S(1)}, f32[7,512]{1,0:T(8,128)S(1)}, u32[]{:S(2)}, u32[]{:S(2)}) collective-permute-start(f32[7,512]{1,0:T(8,128)S(1)} %pad_maximum_fusion.1), channel_id=1, source_target_pairs={{1,0},{2,1},{3,2},{4,3},{5,4},{6,5},{7,6},{8,7},{9,8},{10,9},{11,1... | collective-permute-start | bytes 43016 | tf_op jit(solution)/shard_map/ppermute | solution.py:29
  40.3 0.0 collective-permute-done.7.low
  40.3 0.0 copy-start.4
  40.3 4.1 %collective-permute-done.8.high = f32[7,512]{1,0:T(8,128)S(1)} collective-permute-done((f32[7,512]{1,0:T(8,128)S(1)}, f32[7,512]{1,0:T(8,128)S(1)}, u32[]{:S(2)}, u32[]{:S(2)}) %collective-permute-start.8) | collective-permute-done | bytes 14368 | tf_op jit(solution)/shard_map/ppermute | solution.py:29
  44.4 0.0 copy-start.5
  44.4 0.0 copy-done.4
  44.4 0.6 copy-done.5
  45.0 24.2 %shard_map.105 = f32[4,4096]{1,0:T(4,128)} custom-call(f32[3,4096]{1,0:T(4,128)} %pos.1, f32[4,4096]{1,0:T(4,128)} %charge.1, f32[7,512]{1,0:T(8,128)} %copy-done.4, f32[7,512]{1,0:T(8,128)} %copy-done.5, s32[27,128]{1,0:T(8,128)} %bitcast.16), custom_call_target="tpu_custom_call" | custom-call | tf_op jit(solution)/shard_map/pallas_call | solution.py:179
  69.3 0.0 collective-permute-done.5.low
  69.3 0.0 copy-start.2
  69.3 0.0 collective-permute-done.6.high
  69.3 0.0 copy-done
  69.3 0.6 copy-done.2
  69.9 0.0 copy-start.3
  69.9 0.6 copy-done.3
  70.5 4.8 %shard_map.104 = f32[296,512]{1,0:T(8,128)} custom-call(s32[1]{0:T(128)} %copy.22.live, bf16[296,512]{1,0:T(8,128)(2,1)} %copy-done, bf16[296,32]{1,0:T(8,128)(2,1)} %copy-done.2, bf16[296,32]{1,0:T(8,128)(2,1)} %copy-done.3, s32[8,128]{1,0:T(8,128)} %lists.1, bf16[296,2368]{1,0:T(8,128)(2,1)} %ops.1), custom_call_target="tpu_custom_call" | custom-call | tf_op jit(solution)/shard_map/pallas_call | solution.py:240
  (6 shorter events, 0.1 us)
Async XLA Ops:
  3.1 6.0 %collective-permute-start = (f32[296,64]{1,0:T(8,128)S(1)}, f32[296,64]{1,0:T(8,128)S(1)}, u32[]{:S(2)}, u32[]{:S(2)}) collective-permute-start(f32[296,64]{1,0:T(8,128)S(1)} %broadcast_select_fusion), channel_id=1, source_target_pairs={{0,16},{8,24},{16,0},{24,8},{1,17},{9,25},{17,1},{25,9},{2,18},{10... | collective-permute-start | bytes 227336 | tf_op jit(solution)/shard_map/ppermute | solution.py:36
  9.3 9.1 %collective-permute-start.1 = (f32[296,32]{1,0:T(8,128)S(1)}, f32[296,32]{1,0:T(8,128)S(1)}, u32[]{:S(2)}, u32[]{:S(2)}) collective-permute-start(f32[296,32]{1,0:T(8,128)S(1)} %slice_select_fusion.3), channel_id=1, source_target_pairs={{0,8},{8,0},{16,24},{24,16},{1,9},{9,1},{17,25},{25,17},{2,10},{10... | collective-permute-start | bytes 113672 | tf_op jit(solution)/shard_map/ppermute | solution.py:36
  18.5 12.4 %copy-start.1 = (bf16[296,512]{1,0:T(8,128)(2,1)S(1)}, bf16[296,512]{1,0:T(8,128)(2,1)}, u32[]{:S(2)}) copy-start(bf16[296,512]{1,0:T(8,128)(2,1)} %param.11) | copy-start | bytes 909316
  18.6 4.5 %collective-permute-start.2 = (f32[296,16]{1,0:T(8,128)S(1)}, f32[296,16]{1,0:T(8,128)S(1)}, u32[]{:S(2)}, u32[]{:S(2)}) collective-permute-start(f32[296,16]{1,0:T(8,128)S(1)} %slice_select_fusion.2), channel_id=1, source_target_pairs={{0,4},{1,5},{2,6},{3,7},{4,0},{5,1},{6,2},{7,3},{8,12},{9,13},{10,... | collective-permute-start | bytes 56840 | tf_op jit(solution)/shard_map/ppermute | solution.py:36
  23.3 7.2 %collective-permute-start.3 = (f32[296,8]{1,0:T(8,128)S(1)}, f32[296,8]{1,0:T(8,128)S(1)}, u32[]{:S(2)}, u32[]{:S(2)}) collective-permute-start(f32[296,8]{1,0:T(8,128)S(1)} %slice_select_fusion.1), channel_id=1, source_target_pairs={{0,2},{1,3},{2,0},{3,1},{4,6},{5,7},{6,4},{7,5},{8,10},{9,11},{10,... | collective-permute-start | bytes 28424 | tf_op jit(solution)/shard_map/ppermute | solution.py:36
  23.7 16.6 %collective-permute-start.7 = (f32[7,512]{1,0:T(8,128)S(1)}, f32[7,512]{1,0:T(8,128)S(1)}, u32[]{:S(2)}, u32[]{:S(2)}) collective-permute-start(f32[7,512]{1,0:T(8,128)S(1)} %pad_maximum_fusion), channel_id=1, source_target_pairs={{0,1},{1,2},{2,3},{3,4},{4,5},{5,6},{6,7},{7,8},{8,9},{9,10},{10,1... | collective-permute-start | bytes 43016 | tf_op jit(solution)/shard_map/ppermute | solution.py:26
  30.8 1.4 %collective-permute-start.4 = (f32[296,4]{1,0:T(8,128)S(1)}, f32[296,4]{1,0:T(8,128)S(1)}, u32[]{:S(2)}, u32[]{:S(2)}) collective-permute-start(f32[296,4]{1,0:T(8,128)S(1)} %slice_select_fusion), channel_id=1, source_target_pairs={{0,1},{1,0},{2,3},{3,2},{4,5},{5,4},{6,7},{7,6},{8,9},{9,8},{10,11... | collective-permute-start | bytes 14216 | tf_op jit(solution)/shard_map/ppermute | solution.py:36
  32.5 36.8 %copy-start = (bf16[296,512]{1,0:T(8,128)(2,1)}, bf16[296,512]{1,0:T(8,128)(2,1)S(1)}, u32[]{:S(2)}) copy-start(bf16[296,512]{1,0:T(8,128)(2,1)S(1)} %fusion.owned) | copy-start | bytes 909316
  32.6 36.7 %collective-permute-start.5 = (bf16[296,32]{1,0:T(8,128)(2,1)S(1)}, bf16[296,32]{1,0:T(8,128)(2,1)S(1)}, u32[]{:S(2)}, u32[]{:S(2)}) collective-permute-start(bf16[296,32]{1,0:T(8,128)(2,1)S(1)} %get-tuple-element.3), channel_id=1, source_target_pairs={{0,1},{1,2},{2,3},{3,4},{4,5},{5,6},{6,7},{7,8},{8,9},{9,10},{10,1... | collective-permute-start | bytes 56840 | tf_op jit(solution)/shard_map/ppermute | solution.py:26
  35.6 33.7 %collective-permute-start.6 = (bf16[296,32]{1,0:T(8,128)(2,1)S(1)}, bf16[296,32]{1,0:T(8,128)(2,1)S(1)}, u32[]{:S(2)}, u32[]{:S(2)}) collective-permute-start(bf16[296,32]{1,0:T(8,128)(2,1)S(1)} %get-tuple-element.2), channel_id=1, source_target_pairs={{1,0},{2,1},{3,2},{4,3},{5,4},{6,5},{7,6},{8,7},{9,8},{10,9},{11,1... | collective-permute-start | bytes 56840 | tf_op jit(solution)/shard_map/ppermute | solution.py:29
  37.6 6.9 %collective-permute-start.8 = (f32[7,512]{1,0:T(8,128)S(1)}, f32[7,512]{1,0:T(8,128)S(1)}, u32[]{:S(2)}, u32[]{:S(2)}) collective-permute-start(f32[7,512]{1,0:T(8,128)S(1)} %pad_maximum_fusion.1), channel_id=1, source_target_pairs={{1,0},{2,1},{3,2},{4,3},{5,4},{6,5},{7,6},{8,7},{9,8},{10,9},{11,1... | collective-permute-start | bytes 43016 | tf_op jit(solution)/shard_map/ppermute | solution.py:29
  40.3 4.2 %copy-start.4 = (f32[7,512]{1,0:T(8,128)}, f32[7,512]{1,0:T(8,128)S(1)}, u32[]{:S(2)}) copy-start(f32[7,512]{1,0:T(8,128)S(1)} %collective-permute-done.7.low) | copy-start | bytes 43012
  44.4 0.6 copy-start.5
  69.3 0.6 copy-start.2
  69.9 0.6 copy-start.3

commit v2 on v1

--- a/solution.py
+++ b/solution.py
@@ -1,3 +1,5 @@
+import functools
+
 import jax
 import jax.numpy as jnp
 from jax import lax
@@ -16,24 +18,7 @@
 soften = 0.01
 f32 = jnp.float32
 bf16 = jnp.bfloat16
-
-
-def extended_2(block, sides, width):
-    for axis, dim in sides:
-        count = lax.axis_size(axis)
-        forward = [(i, i + 1) for i in range(count - 1)]
-        backward = [(target, source) for source, target in forward]
-        low = lax.ppermute(
-            lax.slice_in_dim(block, block.shape[dim] - width, None, axis=dim), axis, forward
-        )
-        high = lax.ppermute(lax.slice_in_dim(block, 0, width, axis=dim), axis, backward)
-    return low, high
-
-
-def partner(value, axis, apart):
-    mask = 2**apart
-    pairs = [(source, source ^ mask) for source in range(lax.axis_size(axis))]
-    return lax.ppermute(value, axis, pairs)
+MESH = pl.DeviceIdType.MESH
 
 
 def split3(value):
@@ -144,49 +129,6 @@
     mine = row_ids(flat.shape) % GROUP == lane_ids(flat.shape) // NPT
     flat = jnp.where(mine, flat, f32(0.0))
     out[:, pl.ds(start, size)] = jnp.sum(flat.reshape(Q, GROUP, size), axis=1)
-
-
-def near_kernel(
-    pos, charge, low, high, nbrs, out, coords, charges, sources, targets, counts
-):
-    halo = low.shape[1]
-    count = pos.shape[1]
-    coords[...] = jnp.zeros_like(coords)
-    for ref, at in ((low, 0), (high, halo + count)):
-        coords[0:3, at : at + halo] = ref[0:3, :]
-        charges[:, at : at + halo] = ref[3:, :]
-    coords[0:3, halo : halo + count] = pos[...]
-    charges[:, halo : halo + count] = charge[...]
-    sources[...] = source_rows(coords[...])
-    targets[...] = target_rows(coords[:, halo : halo + count]).T
-    near_counts(nbrs[...], counts)
-    groups = counts.shape[0]
-
-    def step(g, carry):
-        near_group(g, sources, targets, charges, counts, out)
-        return carry
-
-    lax.fori_loop(0, groups, step, 0)
-
-
-def near_field(pos, charge, low, high, nbrs):
-    count = pos.shape[1]
-    halo = low.shape[1]
-    leaves = count // NPT
-    groups = leaves // GROUP
-    span = count + 2 * halo
-    reach = (GROUP + 2 * HL) * NPT
-    return pl.pallas_call(
-        near_kernel,
-        out_shape=jax.ShapeDtypeStruct(charge.shape, f32),
-        scratch_shapes=[
-            pltpu.VMEM((8, span), f32),
-            pltpu.VMEM((Q, span), f32),
-            pltpu.VMEM((64, span), bf16),
-            pltpu.VMEM((count, 64), bf16),
-            pltpu.VMEM((groups, 8, reach), f32),
-        ],
-    )(pos, charge, low, high, nbrs.T)
 
 
 def alive_lanes(live, slots, shape):
@@ -221,76 +163,270 @@
             gathered[o * surface : (o + 2) * surface, b * size : (b + 1) * size] = both
 
 
-def m2l_kernel(live, owned, low, high, lists, ops, out, window, gathered):
-    wide = owned.shape[1]
+def partial_sums(child, users, send, nx, ny):
+    own = SH_DEV * Q
+    rows = send.shape[0]
+    chunks, count = users.shape
+    wide = count * Q
+    row = row_ids((rows, wide))
+    owner = row // own % nx * ny + row // (own * nx)
+    target = owner * own + row % own
+    expand = row_ids((count, wide)) == lane_ids((count, wide)) // Q
+    expand = jnp.where(expand, f32(1.0), f32(0.0)).astype(bf16)
+
+    def chunk_sum(i):
+        ids = users[pl.ds(i, 1), :]
+        both = jnp.concatenate([ids // 256, ids % 256], axis=0)
+        both = jnp.concatenate([both, both, both, both], axis=0)
+        place = jnp.dot(
+            both.astype(f32).astype(bf16), expand, preferred_element_type=f32
+        ).astype(jnp.int32)
+        place = (place[0:1] * 256 + place[1:2]) * Q + lane_ids((1, wide)) % Q
+        hot = jnp.where(target == place, f32(1.0), f32(0.0)).astype(bf16)
+        block = child[:, pl.ds(pl.multiple_of(i * wide, wide), wide)]
+        return lax.dot_general(
+            hot, block, (((1,), (1,)), ((), ())), preferred_element_type=f32
+        )
+
+    send[...] = chunk_sum(0)
+    if chunks > 1:
+
+        def step(i, carry):
+            send[...] += chunk_sum(i)
+            return carry
+
+        lax.fori_loop(1, chunks, step, 0)
+
+
+def fused_kernel(
+    nx,
+    ny,
+    live,
+    child,
+    users,
+    local,
+    pos,
+    charge,
+    nbrs,
+    window,
+    out,
+    send1,
+    recv1,
+    send2,
+    recv2,
+    spread,
+    first,
+    last,
+    low,
+    high,
+    pos_low,
+    pos_high,
+    charge_low,
+    charge_high,
+    coords,
+    charges,
+    sources,
+    targets,
+    counts,
+    send_sem,
+    recv_sem,
+):
+    mx, my = lax.axis_index("gx"), lax.axis_index("gy")
+    total = nx * ny
+    me = mx * ny + my
+    after, before = lax.rem(me + 1, total), lax.rem(me + total - 1, total)
+    after = (after // ny, lax.rem(after, ny))
+    before = (before // ny, lax.rem(before, ny))
+    along_y = [(mx, lax.rem(my + d, ny)) for d in range(1, ny)]
+    along_x = [(lax.rem(mx + d, nx), my) for d in range(1, nx)]
+
+    barrier = pltpu.get_barrier_semaphore()
+    for device in along_y + along_x + [after, before]:
+        pl.semaphore_signal(barrier, inc=1, device_id=device, device_id_type=MESH)
+
+    surface, wide = local.shape
+    slots = wide // Q
     rim = low.shape[1]
-    slots = wide // Q
-    window[:, 0:rim] = low[...]
-    window[:, rim : rim + wide] = owned[...]
-    window[:, rim + wide :] = high[...]
+    halo = pos_low.shape[1]
+    count = pos.shape[1]
+    own = SH_DEV * Q
+    message = nx * own
+    partial_sums(child, users, send1, nx, ny)
+    alive = alive_lanes(live[0], slots, (surface, wide))
+    owned = jnp.where(alive, local[...].astype(f32), f32(0.0)).astype(bf16)
+    last[...] = owned[:, wide - rim :]
+    pl.semaphore_wait(barrier, len(along_y) + len(along_x) + 2)
+
+    at = [0]
+
+    def remote(src, dst, device):
+        k = at[0]
+        at[0] += 1
+        copy = pltpu.make_async_remote_copy(
+            src_ref=src,
+            dst_ref=dst,
+            send_sem=send_sem.at[k],
+            recv_sem=recv_sem.at[k],
+            device_id=device,
+            device_id_type=MESH,
+        )
+        copy.start()
+        return copy
+
+    step1 = []
+    for d in range(1, ny):
+        start = pl.multiple_of(lax.rem(my + d, ny) * message, message)
+        step1.append(
+            remote(send1.at[pl.ds(start, message), :], recv1.at[d - 1], along_y[d - 1])
+        )
+    leaf = [
+        remote(pos.at[:, count - halo : count], pos_low, after),
+        remote(charge.at[:, count - halo : count], charge_low, after),
+        remote(pos.at[:, 0:halo], pos_high, before),
+        remote(charge.at[:, 0:halo], charge_high, before),
+    ]
+    rims = [remote(last, low, after)]
+
+    coords[...] = jnp.zeros_like(coords)
+    coords[0:3, halo : halo + count] = pos[...]
+    charges[:, halo : halo + count] = charge[...]
+    mine = coords[:, halo : halo + count]
+    sources[:, halo : halo + count] = source_rows(mine)
+    targets[...] = target_rows(mine).T
+    near_counts(nbrs[...], counts)
+    groups = counts.shape[0]
+    skip = halo // (GROUP * NPT)
+
+    def step(g, carry):
+        near_group(g, sources, targets, charges, counts, out)
+        return carry
+
+    third = (groups - 2 * skip) // 3
+    lax.fori_loop(skip, skip + third, step, 0)
+
+    for copy in step1:
+        copy.wait()
+    value = send1[pl.ds(pl.multiple_of(my * message, message), message), :]
+    for d in range(ny - 1):
+        value = value + recv1[d]
+    for k in range(nx):
+        send2[k] = value[k * own : (k + 1) * own]
+    step2 = []
+    for d in range(1, nx):
+        step2.append(remote(send2.at[lax.rem(mx + d, nx)], recv2.at[d - 1], along_x[d - 1]))
+
+    lax.fori_loop(skip + third, skip + 2 * third, step, 0)
+
+    for copy in step2:
+        copy.wait()
+    shared = send2[mx]
+    for d in range(nx - 1):
+        shared = shared + recv2[d]
+    spread[...] = jnp.zeros_like(spread)
+    spread[0:own, :] = shared
+    lanes = spread.shape[0]
+    front = local[:, 0:lanes].astype(f32) + spread[...].T
+    front = jnp.where(alive[:, 0:lanes], front, f32(0.0)).astype(bf16)
+    first[...] = front[:, 0:rim]
+    rims.append(remote(first, high, before))
+    window[:, rim : rim + lanes] = front
+    window[:, rim + lanes : rim + wide] = owned[:, lanes:]
+
+    lax.fori_loop(skip + 2 * third, groups - skip, step, 0)
+
+    for copy in leaf:
+        copy.wait()
+    has_low = me > 0
+    has_high = me < total - 1
+    for pos_ref, charge_ref, start, there in (
+        (pos_low, charge_low, 0, has_low),
+        (pos_high, charge_high, halo + count, has_high),
+    ):
+        span = slice(start, start + halo)
+        coords[0:3, span] = pos_ref[...]
+        charges[:, span] = jnp.where(there, charge_ref[...], f32(0.0))
+        sources[:, span] = source_rows(coords[:, span])
+    lax.fori_loop(0, skip, step, 0)
+    lax.fori_loop(groups - skip, groups, step, 0)
+
+    for copy in rims:
+        copy.wait()
+    window[:, 0:rim] = jnp.where(has_low, low[...], jnp.zeros_like(low))
+    window[:, rim + wide :] = jnp.where(has_high, high[...], jnp.zeros_like(high))
+
+
+def fused(live, child, users, local, pos, charge, nbrs):
+    nx, ny = lax.axis_size("gx"), lax.axis_size("gy")
+    surface, wide = local.shape
+    count = pos.shape[1]
+    halo = HL * NPT
+    groups = count // NPT // GROUP
+    span = count + 2 * halo
+    reach = (GROUP + 2 * HL) * NPT
+    rim = wide // 16
+    own = SH_DEV * Q
+    copies = ny - 1 + nx - 1 + 6
+    vmem = pl.BlockSpec(memory_space=pltpu.VMEM)
+    return pl.pallas_call(
+        functools.partial(fused_kernel, nx, ny),
+        out_shape=(
+            jax.ShapeDtypeStruct((surface, wide + 2 * rim), bf16),
+            jax.ShapeDtypeStruct(charge.shape, f32),
+        ),
+        in_specs=[pl.BlockSpec(memory_space=pltpu.SMEM)] + [vmem] * 6,
+        out_specs=(vmem, vmem),
+        scratch_shapes=[
+            pltpu.VMEM((ny * nx * own, surface), f32),
+            pltpu.VMEM((ny - 1, nx * own, surface), f32),
+            pltpu.VMEM((nx, own, surface), f32),
+            pltpu.VMEM((nx - 1, own, surface), f32),
+            pltpu.VMEM((128, surface), f32),
+            pltpu.VMEM((surface, rim), bf16),
+            pltpu.VMEM((surface, rim), bf16),
+            pltpu.VMEM((surface, rim), bf16),
+            pltpu.VMEM((surface, rim), bf16),
+            pltpu.VMEM((3, halo), f32),
+            pltpu.VMEM((3, halo), f32),
+            pltpu.VMEM((Q, halo), f32),
+            pltpu.VMEM((Q, halo), f32),
+            pltpu.VMEM((8, span), f32),
+            pltpu.VMEM((Q, span), f32),
+            pltpu.VMEM((64, span), bf16),
+            pltpu.VMEM((count, 64), bf16),
+            pltpu.VMEM((groups, 8, reach), f32),
+            pltpu.SemaphoreType.DMA((copies,)),
+            pltpu.SemaphoreType.DMA((copies,)),
+        ],
+        compiler_params=pltpu.CompilerParams(collective_id=0, has_side_effects=True),
+    )(live, child, users.reshape(-1, 64), local, pos, charge, nbrs.T)
+
+
+def m2l_kernel(live, window, lists, ops, out, gathered):
     m2l_gather(window, lists[...], gathered)
     result = jnp.dot(ops[...], gathered[...], preferred_element_type=f32)
-    alive = alive_lanes(live[0], slots, result.shape)
+    alive = alive_lanes(live[0], lists.shape[1], result.shape)
     out[...] = jnp.where(alive, result, f32(0.0))
 
 
-def m2l(live, owned, low, high, lists, ops):
-    surface, wide = owned.shape
+def m2l(live, window, lists, ops):
+    surface = window.shape[0]
+    wide = lists.shape[1] * Q
     vmem = pl.BlockSpec(memory_space=pltpu.VMEM)
     return pl.pallas_call(
         m2l_kernel,
         out_shape=jax.ShapeDtypeStruct((surface, wide), f32),
-        in_specs=[pl.BlockSpec(memory_space=pltpu.SMEM)] + [vmem] * 5,
-        scratch_shapes=[
-            pltpu.VMEM((surface, wide + 2 * low.shape[1]), bf16),
-            pltpu.VMEM((surface * lists.shape[0], wide), bf16),
-        ],
-    )(live, owned, low, high, lists, ops)
+        in_specs=[pl.BlockSpec(memory_space=pltpu.SMEM)] + [vmem] * 3,
+        scratch_shapes=[pltpu.VMEM((surface * lists.shape[0], wide), bf16)],
+    )(live, window, lists, ops)
 
 
 def per_device(
     child_dens, users, local_dens, live, m2l_ops, m2l_lists, leaf_pos, leaf_charge, leaf_nbrs
 ):
-    surface = child_dens.shape[0]
-    slots = local_dens.shape[1] // Q
-    shared_total = SH_DEV * lax.axis_size("gx") * lax.axis_size("gy")
-    halo = HL * NPT
-    tail = jnp.concatenate([leaf_pos[:, -halo:], leaf_charge[:, -halo:]], axis=0)
-    head = jnp.concatenate([leaf_pos[:, :halo], leaf_charge[:, :halo]], axis=0)
-    low, high = extended_2(jnp.concatenate([head, tail], axis=1), ((("gx", "gy"), 1),), halo)
-    near_pot = near_field(leaf_pos, leaf_charge, low, high, leaf_nbrs)
-    children = child_dens.reshape(surface, -1, Q)
-    onehot = (users[:, None] == jnp.arange(shared_total, dtype=jnp.int32)[None, :]).astype(
-        jnp.bfloat16
-    )
-    partial_value = jnp.einsum("pcq,cs->psq", children, onehot, preferred_element_type=jnp.float32)
-    block = partial_value.reshape(surface, shared_total * Q)
-    high_rank = lax.axis_index("gx")
-    for bit in range(lax.axis_size("gx").bit_length() - 2, -1, -1):
-        half = block.shape[1] // 2
-        upper = high_rank >> bit & 1 == 1
-        keep = jnp.where(upper, block[:, half:], block[:, :half])
-        give = jnp.where(upper, block[:, :half], block[:, half:])
-        block = keep + partner(give, "gx", bit)
-    low_rank = lax.axis_index("gy")
-    for bit in range(lax.axis_size("gy").bit_length() - 2, -1, -1):
-        half = block.shape[1] // 2
-        upper = low_rank >> bit & 1 == 1
-        keep = jnp.where(upper, block[:, half:], block[:, :half])
-        give = jnp.where(upper, block[:, :half], block[:, half:])
-        block = keep + partner(give, "gy", bit)
-    first = SH_DEV * Q
-    own = local_dens.astype(jnp.float32)
-    own = jnp.concatenate([own[:, :first] + block, own[:, first:]], axis=1)
-    slot_ids = jnp.arange(slots * Q, dtype=jnp.int32) // Q
-    lower = live[0] // 2
-    upper_count = live[0] - lower
-    alive = (slot_ids < lower) | (slot_ids >= slots - upper_count)
-    owned = jnp.where(alive[None, :], own, jnp.float32(0.0)).astype(jnp.bfloat16)
-    rim = slots // 16 * Q
-    wlow, whigh = extended_2(owned, ((("gx", "gy"), 1),), rim)
-    local_exp = m2l(live, owned, wlow, whigh, m2l_lists, m2l_ops)
-    return (local_exp, near_pot)
+    window, near_pot = fused(
+        live, child_dens, users, local_dens, leaf_pos, leaf_charge, leaf_nbrs
+    )
+    return (m2l(live, window, m2l_lists, m2l_ops), near_pot)
 
 
 def solution(mesh):

time: 75.8 us -> 38.8 us (0.51)
  the two profiles are of different devices: /device:TPU:23 before, /device:TPU:0 now
where the time goes in v2:
time: 38.8 us; the launch traced here: 38.6 us
  Pallas kernels  36.7 us (95%)
  between operations  1.29 us (3%)
  local copies, waits for them, and re-layouts  0.63 us (2%)
    pallas_call x1, Pallas kernels, fused(): pl.pallas_call(functools.partial(fused_kernel, nx, ny), out_shape=(jax.Sh...  31.9 us
    pallas_call x1, Pallas kernels, m2l(): pl.pallas_call(m2l_kernel, out_shape=jax.ShapeDtypeStruct((surface, wide)...  4.79 us

profile of v2, /device:TPU:0, one launch (start us, length us, event | category | flops | bytes accessed | tf_op | source)
XLA Modules:
  0.0 38.6 jit_solution(5775504657011055027)
XLA Ops:
  1.3 31.9 %shard_map.104 = (bf16[296,576]{1,0:T(8,128)(2,1)}, f32[4,4096]{1,0:T(4,128)}) custom-call(s32[1]{0:T(128)S(6)} %copy.12.live, bf16[296,256]{1,0:T(8,128)(2,1)} %child.1, s32[1,64]{1,0:T(1,128)} %bitcast.3, bf16[296,512]{1,0:T(8,128)(2,1)} %local.1, f32[3,4096]{1,0:T(4,128)} %pos.1, f32[4,4096]{1,0:T(4,128)} %charge.1, s32[27,128]{1,0:T(8,128)} %bitcast.2), custom_call_target="tpu_custom_call" | custom-call | tf_op jit(solution)/shard_map/pallas_call | solution.py:370
  33.2 0.0 copy-start
  33.2 4.8 %shard_map.105 = f32[296,512]{1,0:T(8,128)} custom-call(s32[1]{0:T(128)S(6)} %copy.12.live, bf16[296,576]{1,0:T(8,128)(2,1)} %get-tuple-element.4.window, s32[8,128]{1,0:T(8,128)} %lists.1, bf16[296,2368]{1,0:T(8,128)(2,1)} %ops.1), custom_call_target="tpu_custom_call" | custom-call | tf_op jit(solution)/shard_map/pallas_call | solution.py:415
  38.0 0.0 copy-done
  38.0 0.6 %copy.13 = f32[4,4096]{1,0:T(4,128)} copy(f32[4,4096]{1,0:T(4,128)S(1)} %copy-done) | data formatting | bytes 131072
Async XLA Ops:
  33.2 4.8 %copy-start = (f32[4,4096]{1,0:T(4,128)S(1)}, f32[4,4096]{1,0:T(4,128)}, u32[]{:S(2)}) copy-start(f32[4,4096]{1,0:T(4,128)} %get-tuple-element.9) | copy-start | bytes 196612

commit v3 on v2

--- a/solution.py
+++ b/solution.py
@@ -12,7 +12,7 @@
 SH_DEV = 1
 NPT = 32
 HL = 16
-GROUP = 4
+GROUP = 8
 BLOCK = 32
 
 soften = 0.01
@@ -79,16 +79,9 @@
     total = jnp.zeros((rows, leaves), f32)
     for j in range(slots):
         total = total + jnp.where(ids == base[j : j + 1, :], f32(1.0), f32(0.0))
-    wide = groups * eight
-    lane = lane_ids((leaves, wide))
-    twice = row_ids((leaves, wide)) == lane // 8 * GROUP + lane % GROUP
-    doubled = jnp.dot(
-        total.astype(bf16), jnp.where(twice, f32(1.0), f32(0.0)).astype(bf16),
-        preferred_element_type=f32,
-    )
     spread = row_ids((rows, reach)) == lane_ids((rows, reach)) // NPT
     full = lax.dot_general(
-        doubled.T.astype(bf16),
+        total.T.astype(bf16),
         jnp.where(spread, f32(1.0), f32(0.0)).astype(bf16),
         (((1,), (0,)), ((), ())),
         preferred_element_type=f32,
@@ -99,33 +92,27 @@
 def near_group(g, sources, targets, charges, counts, out):
     reach = counts.shape[2]
     size = GROUP * NPT
+    rows = Q * GROUP
     start = pl.multiple_of(g * size, size)
-    left = targets[pl.ds(start, size), :]
+    right = targets[:, pl.ds(start, size)]
     cnt = counts[g]
-    half = row_ids(cnt.shape) < GROUP
     ch = charges[:, pl.ds(start, reach)]
-    w = jnp.concatenate(
-        [cnt * jnp.where(half, ch[p : p + 1], ch[p + 1 : p + 2]) for p in range(0, Q, 2)],
-        axis=0,
-    )
+    w = jnp.concatenate([cnt * ch[q : q + 1] for q in range(Q)], axis=0)
     wh = w.astype(bf16)
     wl = (w - wh.astype(f32)).astype(bf16)
     w = jnp.concatenate([wh, wl], axis=0)
-    acc = jnp.zeros((size, w.shape[0]), f32)
-    nt = (((1,), (1,)), ((), ()))
+    total = jnp.zeros((2 * rows, size), f32)
+    extra = jnp.zeros((rows, size), f32)
     for at in range(0, reach, 256):
         width = min(256, reach - at)
-        right = sources[:, pl.ds(pl.multiple_of(start + at, size), width)]
-        dist = jnp.dot(left, right, preferred_element_type=f32)
-        kernel = lax.rsqrt(dist)
+        left = sources[pl.ds(pl.multiple_of(start + at, size), width), :]
+        kernel = lax.rsqrt(jnp.dot(left, right, preferred_element_type=f32))
         high = kernel.astype(bf16)
         low = (kernel - high.astype(f32)).astype(bf16)
-        part = w[:, at : at + width]
-        acc = acc + lax.dot_general(high, part, nt, preferred_element_type=f32)
-        acc = acc + lax.dot_general(low, part, nt, preferred_element_type=f32)
-    flat = acc.T
-    rows = Q * GROUP
-    flat = flat[:rows] + flat[rows:]
+        span = slice(at, at + width)
+        total = total + jnp.dot(w[:, span], high, preferred_element_type=f32)
+        extra = extra + jnp.dot(wh[:, span], low, preferred_element_type=f32)
+    flat = total[:rows] + total[rows:] + extra
     mine = row_ids(flat.shape) % GROUP == lane_ids(flat.shape) // NPT
     flat = jnp.where(mine, flat, f32(0.0))
     out[:, pl.ds(start, size)] = jnp.sum(flat.reshape(Q, GROUP, size), axis=1)
@@ -291,8 +278,8 @@
     coords[0:3, halo : halo + count] = pos[...]
     charges[:, halo : halo + count] = charge[...]
     mine = coords[:, halo : halo + count]
-    sources[:, halo : halo + count] = source_rows(mine)
-    targets[...] = target_rows(mine).T
+    sources[halo : halo + count, :] = source_rows(mine).T
+    targets[...] = target_rows(mine)
     near_counts(nbrs[...], counts)
     groups = counts.shape[0]
     skip = halo // (GROUP * NPT)
@@ -345,7 +332,7 @@
         span = slice(start, start + halo)
         coords[0:3, span] = pos_ref[...]
         charges[:, span] = jnp.where(there, charge_ref[...], f32(0.0))
-        sources[:, span] = source_rows(coords[:, span])
+        sources[span, :] = source_rows(coords[:, span]).T
     lax.fori_loop(0, skip, step, 0)
     lax.fori_loop(groups - skip, groups, step, 0)
 
@@ -391,9 +378,9 @@
             pltpu.VMEM((Q, halo), f32),
             pltpu.VMEM((8, span), f32),
             pltpu.VMEM((Q, span), f32),
-            pltpu.VMEM((64, span), bf16),
-            pltpu.VMEM((count, 64), bf16),
-            pltpu.VMEM((groups, 8, reach), f32),
+            pltpu.VMEM((span, 64), bf16),
+            pltpu.VMEM((64, count), bf16),
+            pltpu.VMEM((groups, GROUP, reach), f32),
             pltpu.SemaphoreType.DMA((copies,)),
             pltpu.SemaphoreType.DMA((copies,)),
         ],

time: 38.8 us -> 28.7 us (0.74)
  Pallas kernels: 36.7 us -> 26.6 us
    pallas_call x1, Pallas kernels: 31.9 us -> 21.8 us  [fused(): pl.pallas_call(functools.partial(fused_kernel, nx, ny), out_shape=(jax.Sh...]
where the time goes in v3:
time: 28.7 us; the launch traced here: 28.6 us
  Pallas kernels  26.6 us (93%)
  between operations  1.29 us (4%)
  local copies, waits for them, and re-layouts  0.63 us (2%)
    pallas_call x1, Pallas kernels, fused(): pl.pallas_call(functools.partial(fused_kernel, nx, ny), out_shape=(jax.Sh...  21.8 us
    pallas_call x1, Pallas kernels, m2l(): pl.pallas_call(m2l_kernel, out_shape=jax.ShapeDtypeStruct((surface, wide)...  4.79 us
    unnamed x3, local copies, waits for them, and re-layouts  0.63 us

profile of v3, /device:TPU:0, one launch (start us, length us, event | category | flops | bytes accessed | tf_op | source)
XLA Modules:
  0.0 28.6 jit_solution(16889164399477434208)
XLA Ops:
  1.3 21.8 %shard_map.104 = (bf16[296,576]{1,0:T(8,128)(2,1)}, f32[4,4096]{1,0:T(4,128)}) custom-call(s32[1]{0:T(128)S(6)} %copy.12.live, bf16[296,256]{1,0:T(8,128)(2,1)} %child.1, s32[1,64]{1,0:T(1,128)} %bitcast.3, bf16[296,512]{1,0:T(8,128)(2,1)} %local.1, f32[3,4096]{1,0:T(4,128)} %pos.1, f32[4,4096]{1,0:T(4,128)} %charge.1, s32[27,128]{1,0:T(8,128)} %bitcast.2), custom_call_target="tpu_custom_call" | custom-call | tf_op jit(solution)/shard_map/pallas_call | solution.py:357
  23.1 0.0 copy-start
  23.1 4.8 %shard_map.105 = f32[296,512]{1,0:T(8,128)} custom-call(s32[1]{0:T(128)S(6)} %copy.12.live, bf16[296,576]{1,0:T(8,128)(2,1)} %get-tuple-element.4.window, s32[8,128]{1,0:T(8,128)} %lists.1, bf16[296,2368]{1,0:T(8,128)(2,1)} %ops.1), custom_call_target="tpu_custom_call" | custom-call | tf_op jit(solution)/shard_map/pallas_call | solution.py:402
  27.9 0.0 copy-done
  27.9 0.6 %copy.13 = f32[4,4096]{1,0:T(4,128)} copy(f32[4,4096]{1,0:T(4,128)S(1)} %copy-done) | data formatting | bytes 131072
Async XLA Ops:
  23.1 4.8 %copy-start = (f32[4,4096]{1,0:T(4,128)S(1)}, f32[4,4096]{1,0:T(4,128)}, u32[]{:S(2)}) copy-start(f32[4,4096]{1,0:T(4,128)} %get-tuple-element.9) | copy-start | bytes 196612

commit v4 on v3

--- a/solution.py
+++ b/solution.py
@@ -102,7 +102,6 @@
     wl = (w - wh.astype(f32)).astype(bf16)
     w = jnp.concatenate([wh, wl], axis=0)
     total = jnp.zeros((2 * rows, size), f32)
-    extra = jnp.zeros((rows, size), f32)
     for at in range(0, reach, 256):
         width = min(256, reach - at)
         left = sources[pl.ds(pl.multiple_of(start + at, size), width), :]
@@ -111,8 +110,8 @@
         low = (kernel - high.astype(f32)).astype(bf16)
         span = slice(at, at + width)
         total = total + jnp.dot(w[:, span], high, preferred_element_type=f32)
-        extra = extra + jnp.dot(wh[:, span], low, preferred_element_type=f32)
-    flat = total[:rows] + total[rows:] + extra
+        total = total + jnp.dot(w[:, span], low, preferred_element_type=f32)
+    flat = total[:rows] + total[rows:]
     mine = row_ids(flat.shape) % GROUP == lane_ids(flat.shape) // NPT
     flat = jnp.where(mine, flat, f32(0.0))
     out[:, pl.ds(start, size)] = jnp.sum(flat.reshape(Q, GROUP, size), axis=1)
@@ -141,12 +140,12 @@
         block = window[:, b * size : b * size + depth]
         ids = row_ids((depth, size)) + b * size
         for o in range(0, offsets, 2):
-            pair = []
-            for k in (o, o + 1):
-                hit = ids == place[k : k + 1, b * size : (b + 1) * size]
-                hot = jnp.where(hit, f32(1.0), f32(0.0)).astype(bf16)
-                pair.append(jnp.dot(block, hot, preferred_element_type=f32))
-            both = jnp.concatenate(pair, axis=0).astype(bf16)
+            hits = [
+                ids == place[k : k + 1, b * size : (b + 1) * size] for k in (o, o + 1)
+            ]
+            hot = jnp.concatenate([jnp.where(hit, f32(1.0), f32(0.0)) for hit in hits], axis=1)
+            pair = jnp.dot(block, hot.astype(bf16), preferred_element_type=f32)
+            both = jnp.concatenate([pair[:, :size], pair[:, size:]], axis=0).astype(bf16)
             gathered[o * surface : (o + 2) * surface, b * size : (b + 1) * size] = both
 
 
@@ -289,7 +288,7 @@
         return carry
 
     third = (groups - 2 * skip) // 3
-    lax.fori_loop(skip, skip + third, step, 0)
+    lax.fori_loop(skip, skip + third, step, 0, unroll=2)
 
     for copy in step1:
         copy.wait()
@@ -302,7 +301,7 @@
     for d in range(1, nx):
         step2.append(remote(send2.at[lax.rem(mx + d, nx)], recv2.at[d - 1], along_x[d - 1]))
 
-    lax.fori_loop(skip + third, skip + 2 * third, step, 0)
+    lax.fori_loop(skip + third, skip + 2 * third, step, 0, unroll=2)
 
     for copy in step2:
         copy.wait()
@@ -319,7 +318,7 @@
     window[:, rim : rim + lanes] = front
     window[:, rim + lanes : rim + wide] = owned[:, lanes:]
 
-    lax.fori_loop(skip + 2 * third, groups - skip, step, 0)
+    lax.fori_loop(skip + 2 * third, groups - skip, step, 0, unroll=2)
 
     for copy in leaf:
         copy.wait()
@@ -333,8 +332,8 @@
         coords[0:3, span] = pos_ref[...]
         charges[:, span] = jnp.where(there, charge_ref[...], f32(0.0))
         sources[span, :] = source_rows(coords[:, span]).T
-    lax.fori_loop(0, skip, step, 0)
-    lax.fori_loop(groups - skip, groups, step, 0)
+    lax.fori_loop(0, skip, step, 0, unroll=2)
+    lax.fori_loop(groups - skip, groups, step, 0, unroll=2)
 
     for copy in rims:
         copy.wait()
@@ -388,23 +387,36 @@
     )(live, child, users.reshape(-1, 64), local, pos, charge, nbrs.T)
 
 
-def m2l_kernel(live, window, lists, ops, out, gathered):
+def m2l_kernel(live, window, lists, ops, near, out, near_out, gathered, held, sem):
+    fetch = pltpu.make_async_copy(ops, held, sem)
+    fetch.start()
+    near_out[...] = near[...]
     m2l_gather(window, lists[...], gathered)
-    result = jnp.dot(ops[...], gathered[...], preferred_element_type=f32)
+    fetch.wait()
+    result = jnp.dot(held[...], gathered[...], preferred_element_type=f32)
     alive = alive_lanes(live[0], lists.shape[1], result.shape)
     out[...] = jnp.where(alive, result, f32(0.0))
 
 
-def m2l(live, window, lists, ops):
+def m2l(live, window, lists, ops, near):
     surface = window.shape[0]
     wide = lists.shape[1] * Q
     vmem = pl.BlockSpec(memory_space=pltpu.VMEM)
     return pl.pallas_call(
         m2l_kernel,
-        out_shape=jax.ShapeDtypeStruct((surface, wide), f32),
-        in_specs=[pl.BlockSpec(memory_space=pltpu.SMEM)] + [vmem] * 3,
-        scratch_shapes=[pltpu.VMEM((surface * lists.shape[0], wide), bf16)],
-    )(live, window, lists, ops)
+        out_shape=(
+            jax.ShapeDtypeStruct((surface, wide), f32),
+            jax.ShapeDtypeStruct(near.shape, f32),
+        ),
+        in_specs=[pl.BlockSpec(memory_space=pltpu.SMEM)] + [vmem] * 2
+        + [pl.BlockSpec(memory_space=pl.ANY), vmem],
+        out_specs=(vmem, vmem),
+        scratch_shapes=[
+            pltpu.VMEM((surface * lists.shape[0], wide), bf16),
+            pltpu.VMEM(ops.shape, bf16),
+            pltpu.SemaphoreType.DMA,
+        ],
+    )(live, window, lists, ops, near)
 
 
 def per_device(
@@ -413,7 +425,7 @@
     window, near_pot = fused(
         live, child_dens, users, local_dens, leaf_pos, leaf_charge, leaf_nbrs
     )
-    return (m2l(live, window, m2l_lists, m2l_ops), near_pot)
+    return m2l(live, window, m2l_lists, m2l_ops, near_pot)
 
 
 def solution(mesh):

time: 28.7 us -> 25.6 us (0.89)
  Pallas kernels: 26.6 us -> 24.2 us
  local copies, waits for them, and re-layouts: 0.63 us -> 0 us
    pallas_call x1, Pallas kernels: 21.8 us -> 20 us  [fused(): pl.pallas_call(functools.partial(fused_kernel, nx, ny), out_shape=(jax.Sh...]
    unnamed x3 -> x0, local copies, waits for them, and re-layouts: 0.63 us -> none
    pallas_call x1, Pallas kernels: 4.79 us -> 4.17 us  [m2l(): pl.pallas_call(m2l_kernel, out_shape=(jax.ShapeDtypeStruct((surface, wide...]
where the time goes in v4:
time: 25.6 us; the launch traced here: 25.4 us
  Pallas kernels  24.2 us (95%)
  between operations  1.29 us (5%)
    pallas_call x1, Pallas kernels, fused(): pl.pallas_call(functools.partial(fused_kernel, nx, ny), out_shape=(jax.Sh...  20 us
    pallas_call x1, Pallas kernels, m2l(): pl.pallas_call(m2l_kernel, out_shape=(jax.ShapeDtypeStruct((surface, wide...  4.17 us

profile of v4, /device:TPU:0, one launch (start us, length us, event | category | flops | bytes accessed | tf_op | source)
XLA Modules:
  0.0 25.4 jit_solution(14665547984994490133)
XLA Ops:
  1.3 20.0 %shard_map.104 = (bf16[296,576]{1,0:T(8,128)(2,1)}, f32[4,4096]{1,0:T(4,128)}) custom-call(s32[1]{0:T(128)S(6)} %copy.11.live, bf16[296,256]{1,0:T(8,128)(2,1)} %child.1, s32[1,64]{1,0:T(1,128)} %bitcast.3, bf16[296,512]{1,0:T(8,128)(2,1)} %local.1, f32[3,4096]{1,0:T(4,128)} %pos.1, f32[4,4096]{1,0:T(4,128)} %charge.1, s32[27,128]{1,0:T(8,128)} %bitcast.2), custom_call_target="tpu_custom_call" | custom-call | tf_op jit(solution)/shard_map/pallas_call | solution.py:356
  21.3 4.2 %shard_map.105 = (f32[296,512]{1,0:T(8,128)}, f32[4,4096]{1,0:T(4,128)}) custom-call(s32[1]{0:T(128)S(6)} %copy.11.live, bf16[296,576]{1,0:T(8,128)(2,1)} %get-tuple-element.4.window, s32[8,128]{1,0:T(8,128)} %lists.1, bf16[296,2368]{1,0:T(8,128)(2,1)} %ops.1, f32[4,4096]{1,0:T(4,128)} %get-tuple-element.5.near), custom_call_target="tpu_custom_call" | custom-call | tf_op jit(solution)/shard_map/pallas_call | solution.py:405

commit v5 on v4

--- a/solution.py
+++ b/solution.py
@@ -288,7 +288,7 @@
         return carry
 
     third = (groups - 2 * skip) // 3
-    lax.fori_loop(skip, skip + third, step, 0, unroll=2)
+    lax.fori_loop(skip, skip + third, step, 0, unroll=4)
 
     for copy in step1:
         copy.wait()
@@ -301,7 +301,7 @@
     for d in range(1, nx):
         step2.append(remote(send2.at[lax.rem(mx + d, nx)], recv2.at[d - 1], along_x[d - 1]))
 
-    lax.fori_loop(skip + third, skip + 2 * third, step, 0, unroll=2)
+    lax.fori_loop(skip + third, skip + 2 * third, step, 0, unroll=4)
 
     for copy in step2:
         copy.wait()
@@ -318,7 +318,7 @@
     window[:, rim : rim + lanes] = front
     window[:, rim + lanes : rim + wide] = owned[:, lanes:]
 
-    lax.fori_loop(skip + 2 * third, groups - skip, step, 0, unroll=2)
+    lax.fori_loop(skip + 2 * third, groups - skip, step, 0, unroll=4)
 
     for copy in leaf:
         copy.wait()

time: 25.6 us -> 25.2 us (0.984)
  Pallas kernels: 24.2 us -> 23.7 us
    pallas_call x1, Pallas kernels: 20 us -> 19.5 us  [fused(): pl.pallas_call(functools.partial(fused_kernel, nx, ny), out_shape=(jax.Sh...]
where the time goes in v5:
time: 25.2 us; the launch traced here: 25 us
  Pallas kernels  23.7 us (94%)
  between operations  1.29 us (5%)
    pallas_call x1, Pallas kernels, fused(): pl.pallas_call(functools.partial(fused_kernel, nx, ny), out_shape=(jax.Sh...  19.5 us
    pallas_call x1, Pallas kernels, m2l(): pl.pallas_call(m2l_kernel, out_shape=(jax.ShapeDtypeStruct((surface, wide...  4.17 us

profile of v5, /device:TPU:0, one launch (start us, length us, event | category | flops | bytes accessed | tf_op | source)
XLA Modules:
  0.0 25.0 jit_solution(9993489379261610633)
XLA Ops:
  1.3 19.5 %shard_map.104 = (bf16[296,576]{1,0:T(8,128)(2,1)}, f32[4,4096]{1,0:T(4,128)}) custom-call(s32[1]{0:T(128)S(6)} %copy.11.live, bf16[296,256]{1,0:T(8,128)(2,1)} %child.1, s32[1,64]{1,0:T(1,128)} %bitcast.3, bf16[296,512]{1,0:T(8,128)(2,1)} %local.1, f32[3,4096]{1,0:T(4,128)} %pos.1, f32[4,4096]{1,0:T(4,128)} %charge.1, s32[27,128]{1,0:T(8,128)} %bitcast.2), custom_call_target="tpu_custom_call" | custom-call | tf_op jit(solution)/shard_map/pallas_call | solution.py:356
  20.8 4.2 %shard_map.105 = (f32[296,512]{1,0:T(8,128)}, f32[4,4096]{1,0:T(4,128)}) custom-call(s32[1]{0:T(128)S(6)} %copy.11.live, bf16[296,576]{1,0:T(8,128)(2,1)} %get-tuple-element.4.window, s32[8,128]{1,0:T(8,128)} %lists.1, bf16[296,2368]{1,0:T(8,128)(2,1)} %ops.1, f32[4,4096]{1,0:T(4,128)} %get-tuple-element.5.near), custom_call_target="tpu_custom_call" | custom-call | tf_op jit(solution)/shard_map/pallas_call | solution.py:405

commit v6 on v5

--- a/solution.py
+++ b/solution.py
@@ -123,7 +123,7 @@
     return (slot < lower) | (slot >= slots - (live - lower))
 
 
-def m2l_gather(window, lists, gathered):
+def m2l_gather(window, lists, gathered, ready):
     offsets, slots = lists.shape
     surface = window.shape[0]
     wide = slots * Q
@@ -147,6 +147,8 @@
             pair = jnp.dot(block, hot.astype(bf16), preferred_element_type=f32)
             both = jnp.concatenate([pair[:, :size], pair[:, size:]], axis=0).astype(bf16)
             gathered[o * surface : (o + 2) * surface, b * size : (b + 1) * size] = both
+        if b % 2 == 1:
+            ready((b - 1) * size, 2 * size)
 
 
 def partial_sums(child, users, send, nx, ny):
@@ -387,15 +389,27 @@
     )(live, child, users.reshape(-1, 64), local, pos, charge, nbrs.T)
 
 
-def m2l_kernel(live, window, lists, ops, near, out, near_out, gathered, held, sem):
+def m2l_kernel(live, window, lists, ops, near, out, near_out, gathered, held, staged, sem, out_sem):
     fetch = pltpu.make_async_copy(ops, held, sem)
     fetch.start()
     near_out[...] = near[...]
-    m2l_gather(window, lists[...], gathered)
-    fetch.wait()
-    result = jnp.dot(held[...], gathered[...], preferred_element_type=f32)
-    alive = alive_lanes(live[0], lists.shape[1], result.shape)
-    out[...] = jnp.where(alive, result, f32(0.0))
+    copies = []
+
+    def ready(start, size):
+        if start == 0:
+            fetch.wait()
+        span = slice(start, start + size)
+        result = jnp.dot(held[...], gathered[:, span], preferred_element_type=f32)
+        alive = alive_lanes(live[0], lists.shape[1], staged.shape)[:, span]
+        staged[:, span] = jnp.where(alive, result, f32(0.0))
+        copies.append(
+            pltpu.make_async_copy(staged.at[:, span], out.at[:, span], out_sem.at[len(copies)])
+        )
+        copies[-1].start()
+
+    m2l_gather(window, lists[...], gathered, ready)
+    for copy in copies:
+        copy.wait()
 
 
 def m2l(live, window, lists, ops, near):
@@ -410,11 +424,13 @@
         ),
         in_specs=[pl.BlockSpec(memory_space=pltpu.SMEM)] + [vmem] * 2
         + [pl.BlockSpec(memory_space=pl.ANY), vmem],
-        out_specs=(vmem, vmem),
+        out_specs=(pl.BlockSpec(memory_space=pl.ANY), vmem),
         scratch_shapes=[
             pltpu.VMEM((surface * lists.shape[0], wide), bf16),
             pltpu.VMEM(ops.shape, bf16),
+            pltpu.VMEM((surface, wide), f32),
             pltpu.SemaphoreType.DMA,
+            pltpu.SemaphoreType.DMA((wide // (2 * BLOCK * Q),)),
         ],
     )(live, window, lists, ops, near)
 

time: 25.2 us -> 26.4 us (1.048)
  Pallas kernels: 23.7 us -> 24.9 us
    pallas_call x1, Pallas kernels: 4.17 us -> 5.36 us  [m2l(): pl.pallas_call(m2l_kernel, out_shape=(jax.ShapeDtypeStruct((surface, wide...]
where the time goes in v6:
time: 26.4 us; the launch traced here: 26.2 us
  Pallas kernels  24.9 us (94%)
  between operations  1.29 us (5%)
    pallas_call x1, Pallas kernels, fused(): pl.pallas_call(functools.partial(fused_kernel, nx, ny), out_shape=(jax.Sh...  19.5 us
    pallas_call x1, Pallas kernels, m2l(): pl.pallas_call(m2l_kernel, out_shape=(jax.ShapeDtypeStruct((surface, wide...  5.36 us

profile of v6, /device:TPU:0, one launch (start us, length us, event | category | flops | bytes accessed | tf_op | source)
XLA Modules:
  0.0 26.2 jit_solution(10726394077574367694)
XLA Ops:
  1.3 19.5 %shard_map.104 = (bf16[296,576]{1,0:T(8,128)(2,1)}, f32[4,4096]{1,0:T(4,128)}) custom-call(s32[1]{0:T(128)S(6)} %copy.11.live, bf16[296,256]{1,0:T(8,128)(2,1)} %child.1, s32[1,64]{1,0:T(1,128)} %bitcast.3, bf16[296,512]{1,0:T(8,128)(2,1)} %local.1, f32[3,4096]{1,0:T(4,128)} %pos.1, f32[4,4096]{1,0:T(4,128)} %charge.1, s32[27,128]{1,0:T(8,128)} %bitcast.2), custom_call_target="tpu_custom_call" | custom-call | tf_op jit(solution)/shard_map/pallas_call | solution.py:358
  20.8 5.4 %shard_map.105 = (f32[296,512]{1,0:T(8,128)}, f32[4,4096]{1,0:T(4,128)}) custom-call(s32[1]{0:T(128)S(6)} %copy.11.live, bf16[296,576]{1,0:T(8,128)(2,1)} %get-tuple-element.4.window, s32[8,128]{1,0:T(8,128)} %lists.1, bf16[296,2368]{1,0:T(8,128)(2,1)} %ops.1, f32[4,4096]{1,0:T(4,128)} %get-tuple-element.5.near), custom_call_target="tpu_custom_call" | custom-call | tf_op jit(solution)/shard_map/pallas_call | solution.py:419
